TPU v7x, 128 devices: a whole 4x4x4 slice. The times are simulated.
128 devices in a mesh: gx: 32 (over z_hi, y, x), gy: 4 (over z_lo, core).
Axes of the slice: x: 4, y: 4, z: 4 (z_hi: 2, z_lo: 2; z = z_hi * 2 + z_lo), core: 2. Of those that a mesh axis runs over, the one named last changes fastest.
Arguments:
- potential: float32 [1024, 128, 256], P('gx', 'gy'), may hold values from 0 to 1
- recovery: float32 [1024, 128, 256], P('gx', 'gy'), may hold values from 0 to 1
- fiber: float32 [2, 1024, 128, 256], P(None, 'gx', 'gy'), may hold values from -3.140625 to 3.140625
- sig_long: float32 [256], P(('gx', 'gy')), may hold values from 0.5 to 2
- sig_trans: float32 [256], P(('gx', 'gy')), may hold values from 0.1 to 0.5
- tile_region: int32 [32, 4, 8], P('gx', 'gy'), may hold values from 0 to 255
- tile_tissue: int32 [32, 4, 8], P('gx', 'gy'), may hold values from 0 to 1, as said below
- cot_potential: float32 [1024, 128, 256], P('gx', 'gy'), may hold values from -6 to 6
- cot_recovery: float32 [1024, 128, 256], P('gx', 'gy'), may hold values from -6 to 6
Outputs:
- final_potential: float32 [1024, 128, 256], P('gx', 'gy')
- adjoint_potential: float32 [1024, 128, 256], P('gx', 'gy')
- grad_long: float32 [256], P(('gx', 'gy'))
- grad_trans: float32 [256], P(('gx', 'gy'))
Inputs may be any that keep to these rules, and one draw needn't show every extreme that they name: `tile_tissue`: tissue flag of each tile; at some tile indices along x (walls, never the last index) every tile, across all of y and z, is myocardium; elsewhere myocardium is sparse.
All inputs are finite; a program needn't handle non-finite values.
Results may differ from a plain program's by a relative error of at most 0.000023.
Values sent between devices are 32-bit elements; how exact they have to be, the bound alone decides.
A program may use at most 192 MiB of HBM per device.

v0:
```python
import jax
import jax.numpy as jnp
from jax import lax
from jax.sharding import PartitionSpec as P

STEPS = 4


UNITS = ((1, 0, 0), (0, 1, 0), (0, 0, 1))
PAIRS = ((0, 1, 3), (0, 2, 4), (1, 2, 5))
TIME_STEP = 0.05
KAPPA = 8.0
ALPHA = 0.15
EPS_W = 0.1


def padded_2(shard, sides, width):
    for axis, dim in sides:
        count, length = (lax.axis_size(axis), shard.shape[dim])
        up = [(i, (i + 1) % count) for i in range(count - 1)]
        down = [(j, i) for i, j in up]
        last = lax.slice_in_dim(shard, length - width, length, axis=dim)
        initial = lax.slice_in_dim(shard, 0, width, axis=dim)
        before = lax.ppermute(last, axis, up)
        after = lax.ppermute(initial, axis, down)
        shard = jnp.concatenate([before, shard, after], axis=dim)
    return shard


def shifted(padded, shift):
    sizes = padded.shape[-3:]
    return padded[
        ...,
        1 + shift[0] : sizes[0] - 1 + shift[0],
        1 + shift[1] : sizes[1] - 1 + shift[1],
        1 + shift[2] : sizes[2] - 1 + shift[2],
    ]


def negate(shift):
    return tuple((-part for part in shift))


def combine_shift(left, right, sign):
    return tuple((first + sign * second for first, second in zip(left, right)))


def central(padded, shift):
    return 0.5 * (shifted(padded, shift) - shifted(padded, negate(shift)))


def fiber_parts(theta, phi):
    fib = (jnp.cos(phi) * jnp.cos(theta), jnp.cos(phi) * jnp.sin(theta), jnp.sin(phi))
    squares = [fib[0] * fib[0], fib[1] * fib[1], fib[2] * fib[2]]
    crosses = [fib[0] * fib[1], fib[0] * fib[2], fib[1] * fib[2]]
    return (squares, crosses)


def tensor_of(theta, phi, slong, strans):
    squares, crosses = fiber_parts(theta, phi)
    excess = slong - strans
    parts = [strans + excess * value for value in squares] + [excess * value for value in crosses]
    return jnp.stack(parts)


def diffuse(field_pad, tensor_pad):
    centre = shifted(field_pad, (0, 0, 0))
    total = jnp.zeros_like(centre)
    for slot in range(3):
        unit = UNITS[slot]
        back = negate(unit)
        coeff = tensor_pad[slot]
        middle = shifted(coeff, (0, 0, 0))
        upper = 0.5 * (middle + shifted(coeff, unit))
        lower = 0.5 * (middle + shifted(coeff, back))
        total = (
            total
            + upper * (shifted(field_pad, unit) - centre)
            - lower * (centre - shifted(field_pad, back))
        )
    for first, second, slot in PAIRS:
        coeff = tensor_pad[slot]
        for along, across in ((UNITS[first], UNITS[second]), (UNITS[second], UNITS[first])):
            back = negate(along)
            plus = shifted(coeff, along) * (
                shifted(field_pad, combine_shift(along, across, 1))
                - shifted(field_pad, combine_shift(along, across, -1))
            )
            minus = shifted(coeff, back) * (
                shifted(field_pad, combine_shift(back, across, 1))
                - shifted(field_pad, combine_shift(back, across, -1))
            )
            total = total + 0.25 * (plus - minus)
    return total


def sensitivities(field_pad, adjoint_pad, squares, crosses):
    centre_u = shifted(field_pad, (0, 0, 0))
    centre_l = shifted(adjoint_pad, (0, 0, 0))
    along_long = jnp.zeros_like(centre_u)
    along_trans = jnp.zeros_like(centre_u)
    for slot in range(3):
        unit = UNITS[slot]
        back = negate(unit)
        term = -0.5 * (
            (shifted(field_pad, unit) - centre_u) * (shifted(adjoint_pad, unit) - centre_l)
            + (centre_u - shifted(field_pad, back)) * (centre_l - shifted(adjoint_pad, back))
        )
        along_long = along_long + term * squares[slot]
        along_trans = along_trans + term * (1.0 - squares[slot])
    for first, second, slot in PAIRS:
        term = -(
            central(adjoint_pad, UNITS[first]) * central(field_pad, UNITS[second])
            + central(adjoint_pad, UNITS[second]) * central(field_pad, UNITS[first])
        )
        along_long = along_long + term * crosses[slot - 3]
        along_trans = along_trans - term * crosses[slot - 3]
    return (along_long, along_trans)


def expand_tiles(values, tile):
    sizes = values.shape
    wide = jnp.broadcast_to(
        values[:, None, :, None, :, None], (sizes[0], tile, sizes[1], tile, sizes[2], tile)
    )
    return wide.reshape(sizes[0] * tile, sizes[1] * tile, sizes[2] * tile)


def tile_sums(field, tile):
    sizes = field.shape
    return field.reshape(
        sizes[0] // tile, tile, sizes[1] // tile, tile, sizes[2] // tile, tile
    ).sum(axis=(1, 3, 5))


def region_table(tile_region, count):
    return (tile_region[..., None] == jnp.arange(count, dtype=jnp.int32)).astype(jnp.float32)


def pad_depth(values):
    widths = ((0, 0),) * (values.ndim - 1) + ((1, 1),)
    return jnp.pad(values, widths)


def field_with_rims(field):
    padded = padded_2(field, (("gx", 0), ("gy", 1)), 1)
    return pad_depth(padded)


def local(
    potential,
    recovery,
    fiber,
    sig_long,
    sig_trans,
    tile_region,
    tile_tissue,
    cot_potential,
    cot_recovery,
):
    tile = potential.shape[0] // tile_region.shape[0]
    full_long, full_trans = (
        lax.all_gather(sig_long, ("gx", "gy"), axis=0, tiled=True),
        lax.all_gather(sig_trans, ("gx", "gy"), axis=0, tiled=True),
    )
    tissue = tile_tissue.astype(jnp.float32)
    table = region_table(tile_region, full_long.shape[0])
    slong = expand_tiles(jnp.sum(table * full_long, axis=-1) * tissue, tile)
    strans = expand_tiles(jnp.sum(table * full_trans, axis=-1) * tissue, tile)
    local_tensor = tensor_of(fiber[0], fiber[1], slong, strans)
    tensor_pad = pad_depth(padded_2(local_tensor, (("gx", 1), ("gy", 2)), 1))
    squares, crosses = fiber_parts(fiber[0], fiber[1])
    states = []
    field, slow = (potential, recovery)
    for step in range(STEPS):
        field_pad = field_with_rims(field)
        states.append((field, slow))
        lap = diffuse(field_pad, tensor_pad)
        ionic = -KAPPA * field * (field - ALPHA) * (field - 1.0) - field * slow
        field, slow = (
            field + TIME_STEP * (lap + ionic),
            slow + TIME_STEP * EPS_W * (-slow - KAPPA * field * (field - ALPHA - 1.0)),
        )
    final_potential = field
    adjoint, adjoint_slow = (cot_potential, cot_recovery)
    total_long = jnp.zeros_like(potential)
    total_trans = jnp.zeros_like(potential)
    for step in range(STEPS - 1, -1, -1):
        field, slow = states[step]
        both = jnp.stack([field, adjoint])
        both_pad = pad_depth(padded_2(both, (("gx", 1), ("gy", 2)), 1))
        stored_pad = both_pad[0]
        adjoint_pad = both_pad[1]
        part_long, part_trans = sensitivities(stored_pad, adjoint_pad, squares, crosses)
        total_long = total_long + part_long
        total_trans = total_trans + part_trans
        lap = diffuse(adjoint_pad, tensor_pad)
        slope = -KAPPA * (3.0 * field * field - 2.0 * (ALPHA + 1.0) * field + ALPHA) - slow
        adjoint, adjoint_slow = (
            adjoint
            + TIME_STEP * (lap + slope * adjoint)
            - TIME_STEP * EPS_W * KAPPA * (2.0 * field - ALPHA - 1.0) * adjoint_slow,
            adjoint_slow - TIME_STEP * field * adjoint - TIME_STEP * EPS_W * adjoint_slow,
        )
    scale = TIME_STEP / tile**1.5
    sums_long = tile_sums(total_long, tile) * tissue * scale
    sums_trans = tile_sums(total_trans, tile) * tissue * scale
    partial_long = jnp.sum(table * sums_long[..., None], axis=(0, 1, 2))
    partial_trans = jnp.sum(table * sums_trans[..., None], axis=(0, 1, 2))
    grad_long, grad_trans = (
        lax.psum_scatter(partial_long, ("gx", "gy"), scatter_dimension=0, tiled=True),
        lax.psum_scatter(partial_trans, ("gx", "gy"), scatter_dimension=0, tiled=True),
    )
    return (final_potential, adjoint, grad_long, grad_trans)


def solution(mesh):
    return jax.shard_map(
        local,
        mesh=mesh,
        in_specs=(
            P("gx", "gy", None),
            P("gx", "gy", None),
            P(None, "gx", "gy", None),
            P(("gx", "gy")),
            P(("gx", "gy")),
            P("gx", "gy", None),
            P("gx", "gy", None),
            P("gx", "gy", None),
            P("gx", "gy", None),
        ),
        out_specs=(P("gx", "gy", None), P("gx", "gy", None), P(("gx", "gy")), P(("gx", "gy"))),
        check_vma=False,
    )
```

profile of v0, /device:TPU:1, one launch (start us, length us, event | category | flops | bytes accessed | tf_op | source)
XLA Modules:
  0.0 590.6 jit_solution(11476820684717234203)
XLA Ops:
  1.4 3.9 collective-permute-start.5
  8.4 72.4 %all-reduce.14 = (f32[256]{0:T(256)S(1)}, f32[256]{0:T(256)S(1)}) all-reduce(f32[256]{0:T(256)S(1)} %dynamic-update-slice, f32[256]{0:T(256)S(1)} %dynamic-update-slice.1), channel_id=1, replica_groups=mesh['gx'=32,'gy'=4] {'gx','gy'}, use_global_device_ids=true, to_apply=%add.9 | all-reduce | flops 512 | bytes 4096
  82.6 8.0 %add_dynamic-update-slice_fusion.2 = (f32[6,32,32,256]{3,2,1,0:T(8,128)S(1)}, f32[1,32,32,256]{3,2,1,0:T(8,128)S(1)}) fusion(f32[256]{0:T(256)S(1)} %sub.1038, f32[256]{0:T(256)S(1)} %broadcast_in_dim.32, f32[2,32,32,256]{3,2,1,0:T(8,128)} %param.11), kind=kLoop, calls=%fused_computation.347 | loop fusion | flops 1048575 | bytes 4196352
  90.6 6.9 %add_dynamic-update-slice_fusion.1 = (f32[6,32,32,256]{3,2,1,0:T(8,128)S(1)}, f32[1,32,32,256]{3,2,1,0:T(8,128)S(1)}) fusion(f32[6,32,32,256]{3,2,1,0:T(8,128)S(1)} %get-tuple-element.58, f32[256]{0:T(256)S(1)} %sub.1038, f32[256]{0:T(256)S(1)} %broadcast_in_dim.32, f32[2,32,32,256]{3,2,1,0:T(8,128)S(1)} %copy-done.43), kind=kLoop, calls=%fused_computation.345 | loop fusion | flops 1048576 | bytes 4196352
  97.5 3.5 add_dynamic-update-slice_fusion
  102.2 4.3 multiply_dynamic-update-slice_fusion.1
  106.5 4.3 multiply_dynamic-update-slice_fusion
  112.1 4.0 collective-permute-start
  116.3 2.4 collective-permute-start.7
  118.7 2.4 collective-permute-start.6
  121.4 1.9 collective-permute-start.3
  123.4 3.6 collective-permute-start.2
  127.1 2.3 select_maximum_fusion.36
  130.8 12.7 %select_maximum_fusion = f32[6,34,34,258]{3,2,1,0:T(8,128)} fusion(f32[6,34,1,256]{3,2,1,0:T(1,128)S(1)} %collective-permute-done.3, f32[6,34,1,256]{3,2,1,0:T(1,128)S(1)} %collective-permute-done.2, f32[6,1,32,256]{3,2,1,0:T(8,128)S(1)} %collective-permute-done.1, f32[6,32,32,256]{3,2,1,0:T(8,128)S(1)} %get-tuple-element.50, ...), kind=kLoop, calls=%fused_computation.2 | loop fusion | flops 21473856 | bytes 14260416 | tf_op jit(solution)/shard_map/concatenate | solution.py:26
  143.5 7.6 %slice_bitcast_fusion.12 = (f32[34,34,258]{2,1,0:T(8,128)}, f32[34,34,258]{2,1,0:T(8,128)S(1)}, f32[34,34,258]{2,1,0:T(8,128)S(1)}, f32[34,34,258]{2,1,0:T(8,128...) fusion(f32[6,34,34,258]{3,2,1,0:T(8,128)} %select_maximum_fusion), kind=kLoop, calls=%fused_computation.58 | loop fusion | bytes 14315904 | tf_op jit(solution)/shard_map/squeeze | solution.py:72
  151.1 25.3 %fusion.18 = (f32[32,32,256]{2,1,0:T(8,128)S(1)}, f32[32,32,256]{2,1,0:T(8,128)}, f32[32,32,256]{2,1,0:T(8,128)}, f32[32,32,256]{2,1,0:T(8,128)}, f32[32,32,256]...) fusion(f32[32,32,256]{2,1,0:T(8,128)} %param.9, f32[34,32,256]{2,1,0:T(8,128)} %copy-done.52, ...), kind=kLoop, calls=%fused_computation.94 | loop fusion | flops 23330816 | bytes 43192320 | tf_op jit(solution)/shard_map/add | solution.py:181
  177.8 4.0 collective-permute-start.9
  184.8 5.9 %collective-permute-start.11 = (f32[34,1,256]{2,1,0:T(1,128)S(1)}, f32[34,1,256]{2,1,0:T(1,128)S(1)}, u32[]{:S(2)}, u32[]{:S(2)}) collective-permute-start(f32[34,1,256]{2,1,0:T(1,128)S(1)} %get-tuple-element.104), channel_id=1, source_target_pairs={{0,1},{1,2},{2,3},{4,5},{5,6},{6,7},{8,9},{9,10},{10,11},{12,13},{... | collective-permute-start | bytes 104456 | tf_op jit(solution)/shard_map/ppermute | solution.py:24
  191.3 2.3 select_maximum_fusion.32
  195.5 22.7 %fusion.114 = (f32[32,32,256]{2,1,0:T(8,128)S(1)}, f32[32,32,256]{2,1,0:T(8,128)}) fusion(f32[32,32,256]{2,1,0:T(8,128)} %copy-done.14, f32[32,32,256]{2,1,0:T(8,128)} %get-tuple-element.47, f32[34,34,258]{2,1,0:T(8,128)} %select_maximum_fusion.32, f32[32,32,256]{2,1,0:T(8,128)} %get-tuple-element.46, f32[32,32,256]{2,1,0:T(8,128)} %get-tuple-element.49, ...), kind=kLoop, calls=%fused_computation.203 | loop fusion | flops 20447232 | bytes 40960000 | tf_op jit(solution)/shard_map/add | solution.py:181
  219.5 4.6 collective-permute-start.13
  227.1 5.1 collective-permute-start.15
  233.2 2.3 select_maximum_fusion.28
  235.5 3.5 pad_maximum_fusion.1
  239.0 22.3 %fusion.92 = f32[32,32,256]{2,1,0:T(8,128)} fusion(f32[32,32,256]{2,1,0:T(8,128)} %copy-done.16, f32[32,32,256]{2,1,0:T(8,128)} %get-tuple-element.47, f32[34,34,258]{2,1,0:T(8,128)} %select_maximum_fusion.28, f32[32,32,256]{2,1,0:T(8,128)} %get-tuple-element.46, f32[32,32,256]{2,1,0:T(8,128)} %get-tuple-element.49, f32[34,33,256]{2,1,0:T(8,128)} %get-tuple-element.99, ...), kind=kLoop, calls=%fused_computation.175 | loop fusion | flops 20447232 | bytes 39911424 | tf_op jit(solution)/shard_map/add | solution.py:181
  263.5 4.6 collective-permute-start.20
  271.4 5.3 collective-permute-start.22
  277.9 3.7 select_maximum_fusion.19
  286.2 7.6 %fusion.32 = f32[32,32,256]{2,1,0:T(8,128)S(1)} fusion(f32[32,32,256]{2,1,0:T(8,128)S(1)} %copy-done.49, f32[32,32,256]{2,1,0:T(8,128)S(1)} %copy-done.20, f32[32,32,256]{2,1,0:T(8,128)S(1)} %copy-done.53, f32[34,34,258]{2,1,0:T(8,128)S(1)} %get-tuple-element.77, f32[32,32,256]{2,1,0:T(8,128)S(1)} %copy-done.31, f32[32,32,256]{2,1,0:T(8,128)S(1)} %copy-done.28, ...), kind=kLoop, calls=%fused_computation.108 | loop fusion | flops 23330816 | bytes 46137344 | tf_op jit(solution)/shard_map/sub | solution.py:200
  296.1 4.6 collective-permute-start.24
  305.3 5.1 collective-permute-start.26
  311.8 6.5 %collective-permute-start.17 = (f32[1,32,256]{2,1,0:T(8,128)S(1)}, f32[1,32,256]{2,1,0:T(8,128)S(1)}, u32[]{:S(2)}, u32[]{:S(2)}) collective-permute-start(f32[1,32,256]{2,1,0:T(8,128)S(1)} %get-tuple-element.108), channel_id=1, source_target_pairs={{0,4},{4,8},{8,12},{12,16},{16,20},{20,24},{24,28},{28,32},{32,36}... | collective-permute-start | bytes 98312 | tf_op jit(solution)/shard_map/ppermute | solution.py:24
  318.4 5.2 select_maximum_fusion.14
  328.2 9.2 %fusion.41 = (f32[32,32,256]{2,1,0:T(8,128)S(1)}, f32[32,32,256]{2,1,0:T(8,128)}) fusion(f32[32,32,256]{2,1,0:T(8,128)S(1)} %copy-done.42, f32[32,32,256]{2,1,0:T(8,128)S(1)} %copy-done.18, f32[34,34,258]{2,1,0:T(8,128)S(1)} %get-tuple-element.75, f32[32,32,256]{2,1,0:T(8,128)S(1)} %copy-done.32, f32[32,32,256]{2,1,0:T(8,128)S(1)} %copy-done.29, ...), kind=kLoop, calls=%fused_computation.117 | loop fusion | flops 22806528 | bytes 48234496 | tf_op jit(solution)/shard_map/sub | solution.py:200
  338.7 6.7 %collective-permute-start.28 = (f32[2,1,32,256]{3,2,1,0:T(8,128)S(1)}, f32[2,1,32,256]{3,2,1,0:T(8,128)S(1)}, u32[]{:S(2)}, u32[]{:S(2)}) collective-permute-start(f32[2,1,32,256]{3,2,1,0:T(8,128)S(1)} %get-tuple-element.88), channel_id=1, source_target_pairs={{0,4},{4,8},{8,12},{12,16},{16,20},{20,24},{24,28},{28,32},{32,36}... | collective-permute-start | bytes 196616 | tf_op jit(solution)/shard_map/ppermute | solution.py:24
  347.4 3.6 collective-permute-start.19
  353.1 3.6 collective-permute-start.30
  356.8 2.2 select_maximum_fusion.24
  359.0 3.7 select_maximum_fusion.9
  364.4 9.7 %fusion.163 = (f32[1,32,32,256]{3,2,1,0:T(8,128)}, f32[32,32,256]{2,1,0:T(8,128)}) fusion(f32[32,32,256]{2,1,0:T(8,128)} %get-tuple-element.40, f32[32,32,256]{2,1,0:T(8,128)S(1)} %copy-done.42, f32[32,32,256]{2,1,0:T(8,128)S(1)} %copy-done.18, f32[32,32,256]{2,1,0:T(8,128)S(1)} %get-tuple-element.39, f32[32,32,256]{2,1,0:T(8,128)S(1)} %copy-done.40, ...), kind=kLoop, calls=%fused_computation.334 | loop fusion | flops 20971520 | bytes 47185920 | tf_op jit(solution)/shard_map/stack | solution.py:190
  376.3 6.7 %collective-permute-start.32 = (f32[2,1,32,256]{3,2,1,0:T(8,128)S(1)}, f32[2,1,32,256]{3,2,1,0:T(8,128)S(1)}, u32[]{:S(2)}, u32[]{:S(2)}) collective-permute-start(f32[2,1,32,256]{3,2,1,0:T(8,128)S(1)} %get-tuple-element.86), channel_id=1, source_target_pairs={{0,4},{4,8},{8,12},{12,16},{16,20},{20,24},{24,28},{28,32},{32,36}... | collective-permute-start | bytes 196616 | tf_op jit(solution)/shard_map/ppermute | solution.py:24
  387.5 4.0 collective-permute-start.34
  391.4 24.2 %fusion.70 = f32[32,32,256]{2,1,0:T(8,128)} fusion(f32[32,32,256]{2,1,0:T(8,128)} %fusion.92, f32[32,32,256]{2,1,0:T(8,128)} %get-tuple-element.47, f32[34,34,258]{2,1,0:T(8,128)} %select_maximum_fusion.24, f32[32,32,256]{2,1,0:T(8,128)} %get-tuple-element.46, f32[32,32,256]{2,1,0:T(8,128)} %get-tuple-element.49, f32[34,33,256]{2,1,0:T(8,128)} %get-tuple-element.95, ...), kind=kLoop, calls=%fused_computation.147 | loop fusion | flops 22282240 | bytes 40960000 | tf_op jit(solution)/shard_map/add | solution.py:181
  415.7 5.2 select_maximum_fusion.4
  424.7 10.4 %fusion.59 = f32[32,32,256]{2,1,0:T(8,128)} fusion(f32[32,32,256]{2,1,0:T(8,128)} %param.10, f32[32,32,256]{2,1,0:T(8,128)} %param.9, f32[32,32,256]{2,1,0:T(8,128)} %copy-done.44, f32[32,32,256]{2,1,0:T(8,128)S(1)} %copy-done.15, f32[34,34,258]{2,1,0:T(8,128)S(1)} %get-tuple-element.71, f32[32,32,256]{2,1,0:T(8,128)} %get-tuple-element.47, ...), kind=kLoop, calls=%fused_computation.135 | loop fusion | flops 26476544 | bytes 49283072 | tf_op jit(solution)/shard_map/sub | solution.py:200
  435.2 37.3 %fusion.146 = (f32[256]{0:T(256)S(1)}, f32[32,32,256]{2,1,0:T(8,128)}, f32[32,32,256]{2,1,0:T(8,128)}, f32[32,32,256]{2,1,0:T(8,128)}, f32[32,32,256]{2,1,0:T(8,...) fusion(f32[1,32,32,256]{3,2,1,0:T(8,128)} %copy-done.47, ...), kind=kLoop, calls=%fused_computation.269 | loop fusion | flops 63700736 | bytes 90178560 | tf_op jit(solution)/shard_map/reduce_sum | solution.py:133
  472.6 11.2 %add_reduce_fusion = f32[256]{0:T(256)S(1)} fusion(f32[32,32,256]{2,1,0:T(8,128)} %get-tuple-element.36, f32[32,32,256]{2,1,0:T(8,128)} %get-tuple-element.35, f32[32,32,256]{2,1,0:T(8,128)} %get-tuple-element.34, f32[32,32,256]{2,1,0:T(8,128)} %get-tuple-element.33, f32[32,32,256]{2,1,0:T(8,128)} %get-tuple-element.32, ...), kind=kLoop, calls=%fused_computation.296 | loop fusion | flops 11009792 | bytes 28312576 | tf_op jit(solution)/shard_map/reduce_sum | solution.py:133
  484.2 104.7 %all-reduce.13 = (f32[256]{0:T(256)S(1)}, f32[256]{0:T(256)S(1)}) all-reduce(f32[256]{0:T(256)S(1)} %get-tuple-element.5, f32[256]{0:T(256)S(1)} %get-tuple-element.4), channel_id=2, replica_groups=mesh['gx'=32,'gy'=4] {'gx','gy'}, use_global_device_ids=true, to_apply=%region_5.6.clone | all-reduce | flops 512 | bytes 4096
  (211 shorter events, 65.1 us)
Async XLA Ops:
  1.4 114.7 %collective-permute-start.5 = (f32[1,32,256]{2,1,0:T(8,128)S(1)}, f32[1,32,256]{2,1,0:T(8,128)S(1)}, u32[]{:S(2)}, u32[]{:S(2)}) collective-permute-start(f32[1,32,256]{2,1,0:T(8,128)S(1)} %get-tuple-element.115), channel_id=1, source_target_pairs={{0,4},{4,8},{8,12},{12,16},{16,20},{20,24},{24,28},{28,32},{32,36}... | collective-permute-start | bytes 98312 | tf_op jit(solution)/shard_map/ppermute | solution.py:24
  5.4 110.9 %collective-permute-start.4 = (f32[1,32,256]{2,1,0:T(8,128)S(1)}, f32[1,32,256]{2,1,0:T(8,128)S(1)}, u32[]{:S(2)}, u32[]{:S(2)}) collective-permute-start(f32[1,32,256]{2,1,0:T(8,128)S(1)} %get-tuple-element.114), channel_id=1, source_target_pairs={{4,0},{8,4},{12,8},{16,12},{20,16},{24,20},{28,24},{32,28},{36,32}... | collective-permute-start | bytes 98312 | tf_op jit(solution)/shard_map/ppermute | solution.py:25
  90.6 11.6 %copy-start.45 = (f32[1,32,32,256]{3,2,1,0:T(8,128)}, f32[1,32,32,256]{3,2,1,0:T(8,128)S(1)}, u32[]{:S(2)}) copy-start(f32[1,32,32,256]{3,2,1,0:T(8,128)S(1)} %get-tuple-element.59) | copy-start | bytes 3145732
  110.8 10.3 %collective-permute-start.1 = (f32[6,1,32,256]{3,2,1,0:T(8,128)S(1)}, f32[6,1,32,256]{3,2,1,0:T(8,128)S(1)}, u32[]{:S(2)}, u32[]{:S(2)}) collective-permute-start(f32[6,1,32,256]{3,2,1,0:T(8,128)S(1)} %get-tuple-element.69), channel_id=1, source_target_pairs={{4,0},{8,4},{12,8},{16,12},{20,16},{24,20},{28,24},{32,28},{36,32}... | collective-permute-start | bytes 589832 | tf_op jit(solution)/shard_map/ppermute | solution.py:25
  112.1 9.0 %collective-permute-start = (f32[6,1,32,256]{3,2,1,0:T(8,128)S(1)}, f32[6,1,32,256]{3,2,1,0:T(8,128)S(1)}, u32[]{:S(2)}, u32[]{:S(2)}) collective-permute-start(f32[6,1,32,256]{3,2,1,0:T(8,128)S(1)} %get-tuple-element.68), channel_id=1, source_target_pairs={{0,4},{4,8},{8,12},{12,16},{16,20},{20,24},{24,28},{28,32},{32,36}... | collective-permute-start | bytes 589832 | tf_op jit(solution)/shard_map/ppermute | solution.py:24
  116.3 10.7 %collective-permute-start.7 = (f32[34,1,256]{2,1,0:T(1,128)S(1)}, f32[34,1,256]{2,1,0:T(1,128)S(1)}, u32[]{:S(2)}, u32[]{:S(2)}) collective-permute-start(f32[34,1,256]{2,1,0:T(1,128)S(1)} %get-tuple-element.107), channel_id=1, source_target_pairs={{0,1},{1,2},{2,3},{4,5},{5,6},{6,7},{8,9},{9,10},{10,11},{12,13},{... | collective-permute-start | bytes 104456 | tf_op jit(solution)/shard_map/ppermute | solution.py:24
  118.7 8.3 %collective-permute-start.6 = (f32[34,1,256]{2,1,0:T(1,128)S(1)}, f32[34,1,256]{2,1,0:T(1,128)S(1)}, u32[]{:S(2)}, u32[]{:S(2)}) collective-permute-start(f32[34,1,256]{2,1,0:T(1,128)S(1)} %get-tuple-element.106), channel_id=1, source_target_pairs={{1,0},{2,1},{3,2},{5,4},{6,5},{7,6},{9,8},{10,9},{11,10},{13,12},{... | collective-permute-start | bytes 104456 | tf_op jit(solution)/shard_map/ppermute | solution.py:25
  121.4 9.1 %collective-permute-start.3 = (f32[6,34,1,256]{3,2,1,0:T(1,128)S(1)}, f32[6,34,1,256]{3,2,1,0:T(1,128)S(1)}, u32[]{:S(2)}, u32[]{:S(2)}) collective-permute-start(f32[6,34,1,256]{3,2,1,0:T(1,128)S(1)} %get-tuple-element.67), channel_id=1, source_target_pairs={{1,0},{2,1},{3,2},{5,4},{6,5},{7,6},{9,8},{10,9},{11,10},{13,12},{... | collective-permute-start | bytes 626696 | tf_op jit(solution)/shard_map/ppermute | solution.py:25
  123.4 7.4 %collective-permute-start.2 = (f32[6,34,1,256]{3,2,1,0:T(1,128)S(1)}, f32[6,34,1,256]{3,2,1,0:T(1,128)S(1)}, u32[]{:S(2)}, u32[]{:S(2)}) collective-permute-start(f32[6,34,1,256]{3,2,1,0:T(1,128)S(1)} %get-tuple-element.66), channel_id=1, source_target_pairs={{0,1},{1,2},{2,3},{4,5},{5,6},{6,7},{8,9},{9,10},{10,11},{12,13},{... | collective-permute-start | bytes 626696 | tf_op jit(solution)/shard_map/ppermute | solution.py:24
  151.1 25.3 %copy-start = (f32[34,34,258]{2,1,0:T(8,128)}, f32[34,34,258]{2,1,0:T(8,128)S(1)}, u32[]{:S(2)}) copy-start(f32[34,34,258]{2,1,0:T(8,128)S(1)} %get-tuple-element.62) | copy-start | bytes 3578980
  151.1 25.3 %copy-start.4 = (f32[34,34,258]{2,1,0:T(8,128)}, f32[34,34,258]{2,1,0:T(8,128)S(1)}, u32[]{:S(2)}) copy-start(f32[34,34,258]{2,1,0:T(8,128)S(1)} %get-tuple-element.65) | copy-start | bytes 3578980
  176.5 17.2 %copy-start.14 = (f32[32,32,256]{2,1,0:T(8,128)}, f32[32,32,256]{2,1,0:T(8,128)S(1)}, u32[]{:S(2)}) copy-start(f32[32,32,256]{2,1,0:T(8,128)S(1)} %get-tuple-element.43) | copy-start | bytes 3145732
  176.5 5.3 collective-permute-start.8
  177.8 5.0 collective-permute-start.9
  182.8 7.9 %collective-permute-start.10 = (f32[34,1,256]{2,1,0:T(1,128)S(1)}, f32[34,1,256]{2,1,0:T(1,128)S(1)}, u32[]{:S(2)}, u32[]{:S(2)}) collective-permute-start(f32[34,1,256]{2,1,0:T(1,128)S(1)} %get-tuple-element.105), channel_id=1, source_target_pairs={{1,0},{2,1},{3,2},{5,4},{6,5},{7,6},{9,8},{10,9},{11,10},{13,12},{... | collective-permute-start | bytes 104456 | tf_op jit(solution)/shard_map/ppermute | solution.py:25
  184.8 6.6 %collective-permute-start.11 = (f32[34,1,256]{2,1,0:T(1,128)S(1)}, f32[34,1,256]{2,1,0:T(1,128)S(1)}, u32[]{:S(2)}, u32[]{:S(2)}) collective-permute-start(f32[34,1,256]{2,1,0:T(1,128)S(1)} %get-tuple-element.104), channel_id=1, source_target_pairs={{0,1},{1,2},{2,3},{4,5},{5,6},{6,7},{8,9},{9,10},{10,11},{12,13},{... | collective-permute-start | bytes 104456 | tf_op jit(solution)/shard_map/ppermute | solution.py:24
  218.2 15.0 %copy-start.16 = (f32[32,32,256]{2,1,0:T(8,128)}, f32[32,32,256]{2,1,0:T(8,128)S(1)}, u32[]{:S(2)}) copy-start(f32[32,32,256]{2,1,0:T(8,128)S(1)} %get-tuple-element.41) | copy-start | bytes 3145732
  218.2 5.9 collective-permute-start.12
  219.5 5.6 collective-permute-start.13
  225.1 7.0 %collective-permute-start.14 = (f32[34,1,256]{2,1,0:T(1,128)S(1)}, f32[34,1,256]{2,1,0:T(1,128)S(1)}, u32[]{:S(2)}, u32[]{:S(2)}) collective-permute-start(f32[34,1,256]{2,1,0:T(1,128)S(1)} %get-tuple-element.101), channel_id=1, source_target_pairs={{1,0},{2,1},{3,2},{5,4},{6,5},{7,6},{9,8},{10,9},{11,10},{13,12},{... | collective-permute-start | bytes 104456 | tf_op jit(solution)/shard_map/ppermute | solution.py:25
  227.1 6.1 %collective-permute-start.15 = (f32[34,1,256]{2,1,0:T(1,128)S(1)}, f32[34,1,256]{2,1,0:T(1,128)S(1)}, u32[]{:S(2)}, u32[]{:S(2)}) collective-permute-start(f32[34,1,256]{2,1,0:T(1,128)S(1)} %get-tuple-element.100), channel_id=1, source_target_pairs={{0,1},{1,2},{2,3},{4,5},{5,6},{6,7},{8,9},{9,10},{10,11},{12,13},{... | collective-permute-start | bytes 104456 | tf_op jit(solution)/shard_map/ppermute | solution.py:24
  262.2 5.9 collective-permute-start.21
  263.5 5.9 collective-permute-start.20
  269.5 7.2 %collective-permute-start.23 = (f32[2,34,1,256]{3,2,1,0:T(1,128)S(1)}, f32[2,34,1,256]{3,2,1,0:T(1,128)S(1)}, u32[]{:S(2)}, u32[]{:S(2)}) collective-permute-start(f32[2,34,1,256]{3,2,1,0:T(1,128)S(1)} %get-tuple-element.85), channel_id=1, source_target_pairs={{1,0},{2,1},{3,2},{5,4},{6,5},{7,6},{9,8},{10,9},{11,10},{13,12},{... | collective-permute-start | bytes 208904 | tf_op jit(solution)/shard_map/ppermute | solution.py:25
  271.4 6.4 %collective-permute-start.22 = (f32[2,34,1,256]{3,2,1,0:T(1,128)S(1)}, f32[2,34,1,256]{3,2,1,0:T(1,128)S(1)}, u32[]{:S(2)}, u32[]{:S(2)}) collective-permute-start(f32[2,34,1,256]{3,2,1,0:T(1,128)S(1)} %get-tuple-element.84), channel_id=1, source_target_pairs={{0,1},{1,2},{2,3},{4,5},{5,6},{6,7},{8,9},{9,10},{10,11},{12,13},{... | collective-permute-start | bytes 208904 | tf_op jit(solution)/shard_map/ppermute | solution.py:24
  294.8 5.9 %collective-permute-start.25 = (f32[2,1,32,256]{3,2,1,0:T(8,128)S(1)}, f32[2,1,32,256]{3,2,1,0:T(8,128)S(1)}, u32[]{:S(2)}, u32[]{:S(2)}) collective-permute-start(f32[2,1,32,256]{3,2,1,0:T(8,128)S(1)} %get-tuple-element.91), channel_id=1, source_target_pairs={{4,0},{8,4},{12,8},{16,12},{20,16},{24,20},{28,24},{32,28},{36,32}... | collective-permute-start | bytes 196616 | tf_op jit(solution)/shard_map/ppermute | solution.py:25
  296.1 5.9 %collective-permute-start.24 = (f32[2,1,32,256]{3,2,1,0:T(8,128)S(1)}, f32[2,1,32,256]{3,2,1,0:T(8,128)S(1)}, u32[]{:S(2)}, u32[]{:S(2)}) collective-permute-start(f32[2,1,32,256]{3,2,1,0:T(8,128)S(1)} %get-tuple-element.90), channel_id=1, source_target_pairs={{0,4},{4,8},{8,12},{12,16},{16,20},{20,24},{24,28},{28,32},{32,36}... | collective-permute-start | bytes 196616 | tf_op jit(solution)/shard_map/ppermute | solution.py:24
  300.8 17.5 %copy-start.18 = (f32[32,32,256]{2,1,0:T(8,128)S(1)}, f32[32,32,256]{2,1,0:T(8,128)}, u32[]{:S(2)}) copy-start(f32[32,32,256]{2,1,0:T(8,128)} %copy-done.16) | copy-start | bytes 3145732
  303.4 14.9 %collective-permute-start.27 = (f32[2,34,1,256]{3,2,1,0:T(1,128)S(1)}, f32[2,34,1,256]{3,2,1,0:T(1,128)S(1)}, u32[]{:S(2)}, u32[]{:S(2)}) collective-permute-start(f32[2,34,1,256]{3,2,1,0:T(1,128)S(1)} %get-tuple-element.83), channel_id=1, source_target_pairs={{1,0},{2,1},{3,2},{5,4},{6,5},{7,6},{9,8},{10,9},{11,10},{13,12},{... | collective-permute-start | bytes 208904 | tf_op jit(solution)/shard_map/ppermute | solution.py:25
  305.3 13.0 %collective-permute-start.26 = (f32[2,34,1,256]{3,2,1,0:T(1,128)S(1)}, f32[2,34,1,256]{3,2,1,0:T(1,128)S(1)}, u32[]{:S(2)}, u32[]{:S(2)}) collective-permute-start(f32[2,34,1,256]{3,2,1,0:T(1,128)S(1)} %get-tuple-element.82), channel_id=1, source_target_pairs={{0,1},{1,2},{2,3},{4,5},{5,6},{6,7},{8,9},{9,10},{10,11},{12,13},{... | collective-permute-start | bytes 208904 | tf_op jit(solution)/shard_map/ppermute | solution.py:24
  310.5 34.9 %collective-permute-start.16 = (f32[1,32,256]{2,1,0:T(8,128)S(1)}, f32[1,32,256]{2,1,0:T(8,128)S(1)}, u32[]{:S(2)}, u32[]{:S(2)}) collective-permute-start(f32[1,32,256]{2,1,0:T(8,128)S(1)} %get-tuple-element.109), channel_id=1, source_target_pairs={{4,0},{8,4},{12,8},{16,12},{20,16},{24,20},{28,24},{32,28},{36,32}... | collective-permute-start | bytes 98312 | tf_op jit(solution)/shard_map/ppermute | solution.py:25
  311.8 33.6 %collective-permute-start.17 = (f32[1,32,256]{2,1,0:T(8,128)S(1)}, f32[1,32,256]{2,1,0:T(8,128)S(1)}, u32[]{:S(2)}, u32[]{:S(2)}) collective-permute-start(f32[1,32,256]{2,1,0:T(8,128)S(1)} %get-tuple-element.108), channel_id=1, source_target_pairs={{0,4},{4,8},{8,12},{12,16},{16,20},{20,24},{24,28},{28,32},{32,36}... | collective-permute-start | bytes 98312 | tf_op jit(solution)/shard_map/ppermute | solution.py:24
  325.2 12.1 %copy-start.10 = (f32[34,34,258]{2,1,0:T(8,128)}, f32[34,34,258]{2,1,0:T(8,128)S(1)}, u32[]{:S(2)}) copy-start(f32[34,34,258]{2,1,0:T(8,128)S(1)} %get-tuple-element.75) | copy-start | bytes 3578980
  337.4 27.0 %copy-start.44 = (f32[32,32,256]{2,1,0:T(8,128)}, f32[32,32,256]{2,1,0:T(8,128)S(1)}, u32[]{:S(2)}) copy-start(f32[32,32,256]{2,1,0:T(8,128)S(1)} %get-tuple-element.39) | copy-start | bytes 3145732
  337.4 13.7 %collective-permute-start.29 = (f32[2,1,32,256]{3,2,1,0:T(8,128)S(1)}, f32[2,1,32,256]{3,2,1,0:T(8,128)S(1)}, u32[]{:S(2)}, u32[]{:S(2)}) collective-permute-start(f32[2,1,32,256]{3,2,1,0:T(8,128)S(1)} %get-tuple-element.89), channel_id=1, source_target_pairs={{4,0},{8,4},{12,8},{16,12},{20,16},{24,20},{28,24},{32,28},{36,32}... | collective-permute-start | bytes 196616 | tf_op jit(solution)/shard_map/ppermute | solution.py:25
  338.7 12.4 %collective-permute-start.28 = (f32[2,1,32,256]{3,2,1,0:T(8,128)S(1)}, f32[2,1,32,256]{3,2,1,0:T(8,128)S(1)}, u32[]{:S(2)}, u32[]{:S(2)}) collective-permute-start(f32[2,1,32,256]{3,2,1,0:T(8,128)S(1)} %get-tuple-element.88), channel_id=1, source_target_pairs={{0,4},{4,8},{8,12},{12,16},{16,20},{20,24},{24,28},{28,32},{32,36}... | collective-permute-start | bytes 196616 | tf_op jit(solution)/shard_map/ppermute | solution.py:24
  345.5 11.3 %collective-permute-start.18 = (f32[34,1,256]{2,1,0:T(1,128)S(1)}, f32[34,1,256]{2,1,0:T(1,128)S(1)}, u32[]{:S(2)}, u32[]{:S(2)}) collective-permute-start(f32[34,1,256]{2,1,0:T(1,128)S(1)} %get-tuple-element.97), channel_id=1, source_target_pairs={{1,0},{2,1},{3,2},{5,4},{6,5},{7,6},{9,8},{10,9},{11,10},{13,12},{... | collective-permute-start | bytes 104456 | tf_op jit(solution)/shard_map/ppermute | solution.py:25
  347.4 9.4 %collective-permute-start.19 = (f32[34,1,256]{2,1,0:T(1,128)S(1)}, f32[34,1,256]{2,1,0:T(1,128)S(1)}, u32[]{:S(2)}, u32[]{:S(2)}) collective-permute-start(f32[34,1,256]{2,1,0:T(1,128)S(1)} %get-tuple-element.96), channel_id=1, source_target_pairs={{0,1},{1,2},{2,3},{4,5},{5,6},{6,7},{8,9},{9,10},{10,11},{12,13},{... | collective-permute-start | bytes 104456 | tf_op jit(solution)/shard_map/ppermute | solution.py:24
  351.2 7.8 %collective-permute-start.31 = (f32[2,34,1,256]{3,2,1,0:T(1,128)S(1)}, f32[2,34,1,256]{3,2,1,0:T(1,128)S(1)}, u32[]{:S(2)}, u32[]{:S(2)}) collective-permute-start(f32[2,34,1,256]{3,2,1,0:T(1,128)S(1)} %get-tuple-element.81), channel_id=1, source_target_pairs={{1,0},{2,1},{3,2},{5,4},{6,5},{7,6},{9,8},{10,9},{11,10},{13,12},{... | collective-permute-start | bytes 208904 | tf_op jit(solution)/shard_map/ppermute | solution.py:25
  353.1 5.9 collective-permute-start.30
  374.9 9.9 %collective-permute-start.33 = (f32[2,1,32,256]{3,2,1,0:T(8,128)S(1)}, f32[2,1,32,256]{3,2,1,0:T(8,128)S(1)}, u32[]{:S(2)}, u32[]{:S(2)}) collective-permute-start(f32[2,1,32,256]{3,2,1,0:T(8,128)S(1)} %get-tuple-element.87), channel_id=1, source_target_pairs={{4,0},{8,4},{12,8},{16,12},{20,16},{24,20},{28,24},{32,28},{36,32}... | collective-permute-start | bytes 196616 | tf_op jit(solution)/shard_map/ppermute | solution.py:25
  376.3 8.5 %collective-permute-start.32 = (f32[2,1,32,256]{3,2,1,0:T(8,128)S(1)}, f32[2,1,32,256]{3,2,1,0:T(8,128)S(1)}, u32[]{:S(2)}, u32[]{:S(2)}) collective-permute-start(f32[2,1,32,256]{3,2,1,0:T(8,128)S(1)} %get-tuple-element.86), channel_id=1, source_target_pairs={{0,4},{4,8},{8,12},{12,16},{16,20},{20,24},{24,28},{28,32},{32,36}... | collective-permute-start | bytes 196616 | tf_op jit(solution)/shard_map/ppermute | solution.py:24
  385.6 30.1 %collective-permute-start.35 = (f32[2,34,1,256]{3,2,1,0:T(1,128)}, f32[2,34,1,256]{3,2,1,0:T(1,128)S(1)}, u32[]{:S(2)}, u32[]{:S(2)}) collective-permute-start(f32[2,34,1,256]{3,2,1,0:T(1,128)} %get-tuple-element.79), channel_id=1, source_target_pairs={{1,0},{2,1},{3,2},{5,4},{6,5},{7,6},{9,8},{10,9},{11,10},{13,12},{... | collective-permute-start | bytes 208904 | tf_op jit(solution)/shard_map/ppermute | solution.py:25
  387.5 28.2 %collective-permute-start.34 = (f32[2,34,1,256]{3,2,1,0:T(1,128)S(1)}, f32[2,34,1,256]{3,2,1,0:T(1,128)S(1)}, u32[]{:S(2)}, u32[]{:S(2)}) collective-permute-start(f32[2,34,1,256]{3,2,1,0:T(1,128)S(1)} %get-tuple-element.78), channel_id=1, source_target_pairs={{0,1},{1,2},{2,3},{4,5},{5,6},{6,7},{8,9},{9,10},{10,11},{12,13},{... | collective-permute-start | bytes 208904 | tf_op jit(solution)/shard_map/ppermute | solution.py:24
  435.2 37.4 %copy-start.46 = (f32[1,32,32,256]{3,2,1,0:T(8,128)S(1)}, f32[1,32,32,256]{3,2,1,0:T(8,128)}, u32[]{:S(2)}) copy-start(f32[1,32,32,256]{3,2,1,0:T(8,128)} %copy-done.45) | copy-start | bytes 3145732
  435.2 37.4 %copy-start.48 = (f32[1,32,32,256]{3,2,1,0:T(8,128)S(1)}, f32[1,32,32,256]{3,2,1,0:T(8,128)}, u32[]{:S(2)}) copy-start(f32[1,32,32,256]{3,2,1,0:T(8,128)} %copy-done.47) | copy-start | bytes 3145732
  472.6 11.5 %copy-start.54 = (s32[1,1,8]{2,1,0:T(1,128)S(1)}, s32[1,1,8]{2,1,0:T(1,128)}, u32[]{:S(2)}) copy-start(s32[1,1,8]{2,1,0:T(1,128)} %param.15) | copy-start | bytes 100
  472.6 11.5 %copy-start.55 = (s32[1,1,8]{2,1,0:T(1,128)S(1)}, s32[1,1,8]{2,1,0:T(1,128)}, u32[]{:S(2)}) copy-start(s32[1,1,8]{2,1,0:T(1,128)} %param.14) | copy-start | bytes 100
  (44 other events, 273.9 us)
where the time goes:
time: 600 us; the launch traced here: 591 us
  other arithmetic  261 us (44%)
  blocking collectives  177 us (30%)
  starting transfers between devices  114 us (19%)
  local copies, waits for them, and re-layouts  27.5 us (5%)
  waiting for transfers between devices  8.84 us (1%)
    unnamed x2, blocking collectives  177 us
    add x4, other arithmetic, local(): field + TIME_STEP * (lap + ionic)  94.4 us
    ppermute x18, starting transfers between devices, padded_2(): before = lax.ppermute(last, axis, up)  84.2 us
    reduce_sum x4, other arithmetic, tile_sums(): return field.reshape(sizes[0] // tile, tile, sizes[1] // tile, tile, size...  48.7 us
    concatenate x15, other arithmetic, padded_2(): shard = jnp.concatenate([before, shard, after], axis=dim)  46.9 us
    ppermute x18, starting transfers between devices, padded_2(): after = lax.ppermute(initial, axis, down)  29.5 us
    sub x3, other arithmetic, local(): adjoint + TIME_STEP * (lap + slope * adjoint)  27.2 us
    unnamed x5, other arithmetic  23.8 us
  transfers between devices with their start and end apart: 36, of which 9 were waited for; matrix products, arithmetic and copies ran while one was open for 13% of the time, Pallas kernels for 0%

commit v1 on v0

v1 whole, which is shorter than its diff:
```python
import jax
import jax.numpy as jnp
from jax import lax
from jax.experimental import pallas as pl
from jax.experimental.pallas import tpu as pltpu
from jax.sharding import PartitionSpec as P

MESH = pl.DeviceIdType.MESH
STEPS = 4
DT = 0.05
EPS_W = 0.1
NX, NY, ZL = 32, 32, 128
Y0 = 8
YP = 48
YT = NY // 8
TILE = 32

XX, XY, XZ, YZ, YY, ZZ = range(6)

SIN = (0.9999999954376937, -0.16666657521871267, 0.008333039791882324, -0.0001980823258586027, 2.603293610558432e-06)
COS = (
    0.9999999997626233,
    -0.4999999931520218,
    0.041666634639589036,
    -0.0013888340619260778,
    2.4759088421126325e-05,
    -2.6032335044441285e-07,
)


def poly(z, coefs):
    total = coefs[-1] * z + coefs[-2]
    for value in coefs[-3::-1]:
        total = total * z + value
    return total


def sincos(x):
    t = (1.5707963705062866 - jnp.abs(x)) - 4.371139000186241e-08
    z = t * t
    cosine = t * poly(z, SIN)
    size = poly(z, COS)
    return jnp.where(x < 0.0, -size, size), cosine


def products(theta, phi):
    st, ct = sincos(theta)
    sp, cp = sincos(phi)
    fx, fy, fz = cp * ct, cp * st, sp
    return {XX: fx * fx, YY: fy * fy, ZZ: fz * fz, XY: fx * fy, XZ: fx * fz, YZ: fy * fz}


def lane():
    return lax.broadcasted_iota(jnp.int32, (8, ZL), 1)


def z_up(h0, h1):
    last = lane() == ZL - 1
    r0, r1 = pltpu.roll(h0, ZL - 1, 1), pltpu.roll(h1, ZL - 1, 1)
    return jnp.where(last, r1, r0), jnp.where(last, 0.0, r1)


def z_down(h0, h1, edge=0.0):
    first = lane() == 0
    r0, r1 = pltpu.roll(h0, 1, 1), pltpu.roll(h1, 1, 1)
    return jnp.where(first, edge, r0), jnp.where(first, r0, r1)


def pair(fn):
    return fn(0), fn(1)


def kernel(
    gx_count,
    gy_count,
    pot,
    rec,
    fib,
    cot_p,
    cot_r,
    sig_l,
    sig_t,
    region,
    tissue,
    out_u,
    out_lam,
    out_l,
    out_t,
    u0,
    u1,
    u2,
    u3,
    l4,
    l3,
    l2,
    l1,
    ulast,
    llast,
    w0,
    w1,
    w2,
    w3,
    mu,
    fp,
    dx,
    dy,
    dz,
    dzm,
    ex,
    tt,
    bb,
    py,
    ay,
    ysend,
    yrecv,
    crecv,
    fysend,
    fyrecv,
    eyh,
    dyh,
    pk,
    tinfo,
    trecv,
    g1send,
    g1recv,
    quad,
    rsend,
    rrecv,
    rg,
    sv,
    acc,
    load_sem,
    xs,
    xr,
    fs,
    fr,
    ts,
    tr,
    g1s,
    g1r,
    g2s,
    g2r,
    r1s,
    r1r,
    r2s,
    r2r,
):
    gx, gy = lax.axis_index("gx"), lax.axis_index("gy")
    has = {"l": gx > 0, "r": gx < gx_count - 1, "d": gy > 0, "u": gy < gy_count - 1}
    us = (u0, u1, u2, u3)
    ls = (l4, l3, l2, l1)
    ws = (w0, w1, w2, w3)
    fields = us + ls

    def loads(index, src, dst, padded):
        out = []
        for h in range(2):
            s = src.at[:, :, pl.ds(h * ZL, ZL)]
            d = dst.at[pl.ds(1, NX), h, pl.ds(Y0, NY), :] if padded else dst.at[:, h]
            out.append(pltpu.make_async_copy(s, d, load_sem.at[index, h]))
        return out

    copies = [
        loads(0, pot, u0, True),
        loads(1, cot_p, l4, True),
        loads(2, fib.at[0], tt, False),
        loads(3, fib.at[1], bb, True),
        loads(4, rec, w0, False),
        loads(5, cot_r, mu, False),
    ]
    for group in copies:
        for copy in group:
            copy.start()

    barrier = pltpu.get_barrier_semaphore()

    @pl.loop(1, gx_count)
    def _(k):
        pl.semaphore_signal(barrier, inc=1, device_id=(lax.rem(gx + k, gx_count), gy), device_id_type=MESH)

    @pl.loop(1, gy_count)
    def _(k):
        pl.semaphore_signal(barrier, inc=1, device_id=(gx, lax.rem(gy + k, gy_count)), device_id_type=MESH)

    corner_list = (("l", "d"), ("l", "u"), ("r", "d"), ("r", "u"))
    step_of = {"l": (-1, 0), "r": (1, 0), "d": (0, -1), "u": (0, 1)}

    def both(a, b):
        return jnp.logical_and(has[a], has[b])

    def target(*sides):
        return (gx + sum(step_of[s][0] for s in sides), gy + sum(step_of[s][1] for s in sides))

    for a, b in corner_list:

        @pl.when(both(a, b))
        def _(a=a, b=b):
            pl.semaphore_signal(barrier, inc=1, device_id=target(a, b), device_id_type=MESH)

    gxi = (gx > 0).astype(jnp.int32) + (gx < gx_count - 1).astype(jnp.int32)
    gyi = (gy > 0).astype(jnp.int32) + (gy < gy_count - 1).astype(jnp.int32)

    @pl.when(jnp.logical_not(has["l"]))
    def _():
        for f in fields:
            f[0, :, Y0 : Y0 + NY, :] = jnp.zeros((2, NY, ZL), jnp.float32)
        for c in (XX, XY, XZ):
            fp[c, 0, :, Y0 : Y0 + NY, :] = jnp.zeros((2, NY, ZL), jnp.float32)
        trecv[0] = jnp.zeros((8, ZL), jnp.float32)

    @pl.when(jnp.logical_not(has["r"]))
    def _():
        for f in fields:
            f[NX + 1, :, Y0 : Y0 + NY, :] = jnp.zeros((2, NY, ZL), jnp.float32)
        for c in (XX, XY, XZ):
            fp[c, NX + 1, :, Y0 : Y0 + NY, :] = jnp.zeros((2, NY, ZL), jnp.float32)
        trecv[1] = jnp.zeros((8, ZL), jnp.float32)

    for side, name in enumerate("du"):

        @pl.when(jnp.logical_not(has[name]))
        def _(side=side):
            for k in range(8):
                yrecv[k, side, :, Y0 : Y0 + NY, :] = jnp.zeros((2, NY, ZL), jnp.float32)
            fyrecv[side] = jnp.zeros((3, 2, NX, ZL), jnp.float32)
            trecv[2 + side] = jnp.zeros((8, ZL), jnp.float32)

    for c, (a, b) in enumerate(corner_list):

        @pl.when(jnp.logical_not(both(a, b)))
        def _(c=c):
            for k in range(8):
                crecv[k, c] = jnp.zeros((2, 8, ZL), jnp.float32)

    pl.semaphore_wait(barrier, gx_count - 1 + gy_count - 1 + gxi * gyi)

    def remote(src, dst, send, recv, device):
        return pltpu.make_async_remote_copy(
            src_ref=src, dst_ref=dst, send_sem=send, recv_sem=recv, device_id=device, device_id_type=MESH
        )

    lanes = lane()
    tile_of = lanes // TILE

    def lane_vector(ref, h):
        value = jnp.zeros((8, ZL), jnp.float32)
        for k in range(4):
            value = jnp.where(tile_of == k, ref[0, 0, 4 * h + k].astype(jnp.float32), value)
        return value

    own_r = [lane_vector(region, h) for h in range(2)]
    own_t = [lane_vector(tissue, h) for h in range(2)]
    sub = lax.broadcasted_iota(jnp.int32, (8, ZL), 0)
    subf = sub.astype(jnp.float32)
    tinfo[...] = jnp.where(
        sub == 0, own_r[0], jnp.where(sub == 1, own_r[1], jnp.where(sub == 2, own_t[0], own_t[1]))
    )
    opposite = {"l": 1, "r": 0, "d": 3, "u": 2}
    names = "lrdu"

    def tile_copies():
        return [
            (
                has[s],
                has[names[opposite[s]]],
                remote(tinfo, trecv.at[opposite[s]], ts.at[i], tr.at[opposite[s]], target(s)),
            )
            for i, s in enumerate(names)
        ]

    def start(list_):
        for cond, _, copy in list_:

            @pl.when(cond)
            def _(copy=copy):
                copy.start()

    def wait_recv(list_):
        for _, cond, copy in list_:

            @pl.when(cond)
            def _(copy=copy):
                copy.wait_recv()

    def wait_send(list_):
        for cond, _, copy in list_:

            @pl.when(cond)
            def _(copy=copy):
                copy.wait_send()

    start(tile_copies())

    value = jnp.where(
        lanes < 64, jnp.where(sub == 2 * gy, sig_l[0], sig_l[1]), jnp.where(sub == 2 * gy, sig_t[0], sig_t[1])
    )
    mine = jnp.where(jnp.logical_or(sub == 2 * gy, sub == 2 * gy + 1), value, 0.0)
    g1send[...] = mine

    def g1(k):
        return remote(g1send, g1recv.at[k], g1s.at[k], g1r.at[k], (gx, lax.rem(gy + k, gy_count)))

    for k in range(1, gy_count):
        g1(k).start()

    def exchange(k):
        f = fields[k]
        rows = pl.ds(Y0, NY)
        out = [
            (has["l"], has["r"], remote(f.at[1, :, rows, :], f.at[NX + 1, :, rows, :], xs.at[k, 0], xr.at[k, 1], target("l"))),
            (has["r"], has["l"], remote(f.at[NX, :, rows, :], f.at[0, :, rows, :], xs.at[k, 1], xr.at[k, 0], target("r"))),
            (has["d"], has["u"], remote(ysend.at[k, 0], yrecv.at[k, 1, :, rows, :], xs.at[k, 2], xr.at[k, 3], target("d"))),
            (has["u"], has["d"], remote(ysend.at[k, 1], yrecv.at[k, 0, :, rows, :], xs.at[k, 3], xr.at[k, 2], target("u"))),
        ]
        for c, (a, b) in enumerate(corner_list):
            xrow = 0 if a == "l" else NX - 8
            src = ysend.at[k, 0 if b == "d" else 1, :, pl.ds(xrow, 8), :]
            out.append((both(a, b), both(*corner_list[3 - c]), remote(src, crecv.at[k, 3 - c], xs.at[k, 4 + c], xr.at[k, 7 - c], target(a, b))))
        return out

    def wait_load(index):
        for copy in copies[index]:
            copy.wait()

    def pack_rows(f, k):
        @pl.loop(0, NX)
        def _(x):
            for h in range(2):
                ysend[k, 0, h, pl.ds(x, 1), :] = f[x + 1, h, Y0 : Y0 + 1, :]
                ysend[k, 1, h, pl.ds(x, 1), :] = f[x + 1, h, Y0 + NY - 1 : Y0 + NY, :]

    wait_load(0)
    pack_rows(u0, 0)
    start(exchange(0))
    wait_load(1)
    pack_rows(l4, 4)
    start(exchange(4))

    quad_own = mine
    for k in range(1, gy_count):
        g1(k).wait_recv()
        quad_own = quad_own + g1recv[k]
    quad[0] = quad_own

    def g2(k):
        return remote(quad.at[0], quad.at[k], g2s, g2r, (lax.rem(gx + k, gx_count), gy))

    @pl.loop(1, gx_count)
    def _(k):
        g2(k).start()

    wait_load(2)
    wait_load(3)

    def trig(x):
        for yt in range(YT):
            y = yt * 8
            for h in range(2):
                got = products(tt[x, h, y : y + 8, :], bb[x + 1, h, Y0 + y : Y0 + y + 8, :])
                for c in range(6):
                    fp[c, x + 1, h, Y0 + y : Y0 + y + 8, :] = got[c]
                for i, c in enumerate((XY, YZ, YY)):
                    if yt == 0:
                        fysend[0, i, h, pl.ds(x, 1), :] = got[c][0:1]
                    if yt == YT - 1:
                        fysend[1, i, h, pl.ds(x, 1), :] = got[c][7:8]

    pl.loop(0, NX)(trig)

    def fiber_exchange():
        rows = pl.ds(Y0, NY)
        return [
            (has["l"], has["r"], remote(fp.at[pl.ds(0, 3), 1, :, rows, :], fp.at[pl.ds(0, 3), NX + 1, :, rows, :], fs.at[0], fr.at[1], target("l"))),
            (has["r"], has["l"], remote(fp.at[pl.ds(0, 3), NX, :, rows, :], fp.at[pl.ds(0, 3), 0, :, rows, :], fs.at[1], fr.at[0], target("r"))),
            (has["d"], has["u"], remote(fysend.at[0], fyrecv.at[1], fs.at[2], fr.at[3], target("d"))),
            (has["u"], has["d"], remote(fysend.at[1], fyrecv.at[0], fs.at[3], fr.at[2], target("u"))),
        ]

    start(fiber_exchange())

    wait_recv(tile_copies())
    remote(quad.at[pl.ds(1, gx_count - 1)], quad.at[pl.ds(1, gx_count - 1)], g2s, g2r, (gx, gy)).wait_recv()
    regions = list(own_r)
    flags = list(own_t)
    for i in range(4):
        for h in range(2):
            regions.append(jnp.broadcast_to(trecv[i, h : h + 1, :], (8, ZL)))
            flags.append(jnp.broadcast_to(trecv[i, 2 + h : 3 + h, :], (8, ZL)))

    def lookup(k, sums):
        tile = quad[k]
        turned = pltpu.roll(tile, 64, 1)
        low = lanes < 64
        long_, trans = jnp.where(low, tile, turned), jnp.where(low, turned, tile)
        group = lax.rem(gx - k + gx_count, gx_count)
        ids = subf + (8 * group).astype(jnp.float32)
        new = []
        for i in range(10):
            hit = regions[i] == ids
            new.append(sums[2 * i] + jnp.where(hit, long_, 0.0))
            new.append(sums[2 * i + 1] + jnp.where(hit, trans, 0.0))
        return tuple(new)

    sums = lax.fori_loop(0, gx_count, lookup, tuple(jnp.zeros((8, ZL), jnp.float32) for _ in range(20)))
    for i in range(10):
        s_l = jnp.broadcast_to(jnp.sum(sums[2 * i], axis=0, keepdims=True), (8, ZL)) * flags[i]
        s_t = jnp.broadcast_to(jnp.sum(sums[2 * i + 1], axis=0, keepdims=True), (8, ZL)) * flags[i]
        sv[i // 2, 0, i % 2] = s_t
        sv[i // 2, 1, i % 2] = s_l - s_t

    wait_recv(fiber_exchange())
    c_pair = 0.25 * DT
    c_axis = 0.5 * DT
    st = pair(lambda h: sv[0, 0, h])
    ee = pair(lambda h: sv[0, 1, h])
    ea = pair(lambda h: c_axis * ee[h])
    ep = pair(lambda h: c_pair * ee[h])
    s2 = pair(lambda h: DT * st[h])

    def coefficients(p):
        for yt in range(YT):
            y = yt * 8
            r = slice(Y0 + y, Y0 + y + 8)
            dzz = []
            for h in range(2):
                q = slice(y, y + 8)
                dx[p, h, q, :] = s2[h] + ea[h] * (fp[XX, p, h, r, :] + fp[XX, p + 1, h, r, :])
                up = fp[YY, p, h, Y0 + y + 1 : Y0 + y + 9, :]
                dy[p, h, q, :] = s2[h] + ea[h] * (fp[YY, p, h, r, :] + up)
                dzz.append(c_axis * st[h] + ea[h] * fp[ZZ, p, h, r, :])
                for i, c in enumerate((XY, XZ, YZ)):
                    ex[i, p, h, q, :] = ep[h] * fp[c, p, h, r, :]
            up = z_up(*dzz)
            for h in range(2):
                dz[p, h, y : y + 8, :] = dzz[h] + up[h]
            dzm[p, y : y + 8, :] = dzz[0]

    pl.loop(1, NX + 1)(coefficients)
    for side, plane, inner in ((0, 0, 1), (1, NX + 1, NX)):
        for h in range(2):
            st_n, e_n = sv[1 + side, 0, h], sv[1 + side, 1, h]
            for yt in range(YT):
                q = slice(yt * 8, yt * 8 + 8)
                r = slice(Y0 + yt * 8, Y0 + yt * 8 + 8)
                total = (st_n + e_n * fp[XX, plane, h, r, :]) + (st[h] + ee[h] * fp[XX, inner, h, r, :])
                dx[0 if side == 0 else NX, h, q, :] = c_axis * total
                for i, c in enumerate((XY, XZ)):
                    ex[i, plane, h, q, :] = c_pair * e_n * fp[c, plane, h, r, :]
    for side in range(2):
        for h in range(2):
            st_n, e_n = sv[3 + side, 0, h], sv[3 + side, 1, h]
            for t in range(NX // 8):
                q = slice(t * 8, t * 8 + 8)
                total = (st_n + e_n * fyrecv[side, 2, h, q, :]) + (st[h] + ee[h] * fysend[side, 2, h, q, :])
                dyh[side, h, q, :] = c_axis * total
                for i in range(2):
                    eyh[side, i, h, q, :] = c_pair * e_n * fyrecv[side, i, h, q, :]

    @pl.loop(0, NX)
    def _(x):
        for h in range(2):
            dy[x + 1, h, NY - 1 : NY, :] = dyh[1, h, pl.ds(x, 1), :]

    acc[...] = jnp.zeros_like(acc)

    def install(k):
        f = fields[k]
        for c, (a, b) in enumerate(corner_list):
            plane = 0 if a == "l" else NX + 1
            row = Y0 - 1 if b == "d" else Y0 + NY
            side = 0 if b == "d" else 1
            edge = Y0 - 1 if a == "l" else Y0 + NX
            at = 7 if a == "l" else 0
            for h in range(2):
                v = crecv[k, c, h, at : at + 1, :]
                f[plane, h, row : row + 1, :] = v
                yrecv[k, side, h, edge : edge + 1, :] = v
        for side in range(2):
            for t in range(NX // 8):
                q = slice(t * 8, t * 8 + 8)
                r = slice(Y0 + t * 8, Y0 + t * 8 + 8)
                c = pair(lambda h: yrecv[k, side, h, r, :])
                zp, zm = z_up(*c), z_down(*c)
                for h in range(2):
                    g_x = yrecv[k, side, h, Y0 + t * 8 + 1 : Y0 + t * 8 + 9, :] - yrecv[k, side, h, Y0 + t * 8 - 1 : Y0 + t * 8 + 7, :]
                    flux = eyh[side, 0, h, q, :] * g_x + eyh[side, 1, h, q, :] * (zp[h] - zm[h])
                    if side == 0:
                        flux = flux + dyh[0, h, q, :] * (ysend[k, 0, h, q, :] - c[h])
                    pk[side, h, q, :] = flux

        @pl.loop(0, NX)
        def _(x):
            for h in range(2):
                f[x + 1, h, Y0 - 1 : Y0, :] = yrecv[k, 0, h, pl.ds(x + Y0, 1), :]
                f[x + 1, h, Y0 + NY : Y0 + NY + 1, :] = yrecv[k, 1, h, pl.ds(x + Y0, 1), :]
                ay[x + 1, h, Y0 - 1 : Y0, :] = pk[0, h, pl.ds(x, 1), :]
                py[x + 1, h, Y0 + NY : Y0 + NY + 1, :] = pk[1, h, pl.ds(x, 1), :]

    def rows(y, shift=0):
        return slice(Y0 + y + shift, Y0 + y + shift + 8)

    def edge_flux(f, p, yt):
        y = yt * 8
        q = slice(y, y + 8)
        c = pair(lambda h: f[p, h, rows(y), :])
        zp, zm = z_up(*c), z_down(*c)
        out = []
        for h in range(2):
            g_y = f[p, h, rows(y, 1), :] - f[p, h, rows(y, -1), :]
            out.append(ex[0, p, h, q, :] * g_y + ex[1, p, h, q, :] * (zp[h] - zm[h]))
        return c, out

    def before(f):
        for yt in range(YT):
            y = yt * 8
            c, flux = edge_flux(f, 0, yt)
            for h in range(2):
                bb[0, h, rows(y), :] = flux[h] + dx[0, h, y : y + 8, :] * (f[1, h, rows(y), :] - c[h])

    def stage_a(f, p, yt, react):
        y = yt * 8
        q = slice(y, y + 8)
        c = pair(lambda h: f[p, h, rows(y), :])
        xp = pair(lambda h: f[p + 1, h, rows(y), :])
        xm = pair(lambda h: f[p - 1, h, rows(y), :])
        yp = pair(lambda h: f[p, h, rows(y, 1), :])
        ym = pair(lambda h: f[p, h, rows(y, -1), :])
        zp, zm = z_up(*c), z_down(*c)
        own = react(p, y, c)
        flux_x, local, pz, az = [], [], [], []
        for h in range(2):
            e_xy, e_xz, e_yz = (ex[i, p, h, q, :] for i in range(3))
            g_x, g_y, g_z = xp[h] - xm[h], yp[h] - ym[h], zp[h] - zm[h]
            p_x = e_xy * g_y + e_xz * g_z
            p_y = e_xy * g_x + e_yz * g_z
            p_z = e_xz * g_x + e_yz * g_y
            f_x = dx[p, h, q, :] * (xp[h] - c[h])
            f_y = dy[p, h, q, :] * (yp[h] - c[h])
            f_z = dz[p, h, q, :] * (zp[h] - c[h])
            back = bb[p - 1, h, rows(y), :]
            bb[p, h, rows(y), :] = f_x + p_x
            py[p, h, rows(y), :] = p_y
            ay[p, h, rows(y), :] = f_y + p_y
            pz.append(p_z)
            az.append(f_z + p_z)
            flux_x.append(p_x)
            local.append((own[h] + f_x) + (f_y + f_z) - back)
        up = z_up(*pz)
        down = z_down(*az, edge=dzm[p, q, :] * c[0])
        for h in range(2):
            tt[p - 1, h, q, :] = local[h] + (up[h] - down[h])
        return flux_x

    def stage_b(p, yt, flux_x, put):
        y = yt * 8
        for h in range(2):
            value = (tt[p - 1, h, y : y + 8, :] + flux_x[h]) + (py[p, h, rows(y, 1), :] - ay[p, h, rows(y, -1), :])
            put(p, h, yt, value)

    def apply(k, react, put):
        f = fields[k]
        before(f)
        for yt in range(YT):
            stage_a(f, 1, yt, react)

        @pl.loop(2, NX + 1)
        def _(p):
            for yt in range(YT):
                stage_b(p - 1, yt, stage_a(f, p, yt, react), put)

        for yt in range(YT):
            stage_b(NX, yt, edge_flux(f, NX + 1, yt)[1], put)

    def put_field(k):
        f = fields[k]

        def put(p, h, yt, value):
            f[p, h, rows(yt * 8), :] = value
            if yt == 0:
                ysend[k, 0, h, pl.ds(p - 1, 1), :] = value[0:1]
            if yt == YT - 1:
                ysend[k, 1, h, pl.ds(p - 1, 1), :] = value[7:8]

        return put

    def put_last(ref):
        def put(p, h, yt, value):
            ref[p - 1, h, yt * 8 : yt * 8 + 8, :] = value

        return put

    def store(ref, out, index):
        return [
            pltpu.make_async_copy(ref.at[:, h], out.at[:, :, pl.ds(h * ZL, ZL)], load_sem.at[index, h]) for h in range(2)
        ]

    wait_load(4)
    wait_load(5)
    for n in range(STEPS):
        wait_recv(exchange(n))
        install(n)

        def react(p, y, c, n=n):
            q = slice(y, y + 8)
            out = []
            for h in range(2):
                w = ws[n][p - 1, h, q, :]
                u = c[h]
                rate = (1.0 - DT * w) - (u - 0.15) * (8.0 * DT * u - 8.0 * DT)
                out.append(u * rate)
                if n < STEPS - 1:
                    ws[n + 1][p - 1, h, q, :] = (1.0 - DT * EPS_W) * w - u * (
                        8.0 * DT * EPS_W * u - 8.0 * DT * EPS_W * 1.15
                    )
            return out

        apply(n, react, put_field(n + 1) if n < STEPS - 1 else put_last(ulast))
        if n < STEPS - 1:
            start(exchange(n + 1))
    for copy in store(ulast, out_u, 0):
        copy.start()

    def sens(n, k):
        u, lam = us[n], fields[k]

        def body(p, sums):
            total_l, total_t = [sums[0], sums[1]], [sums[2], sums[3]]
            for yt in range(YT):
                y = yt * 8
                both_ = []
                for f in (u, lam):
                    c = pair(lambda h: f[p, h, rows(y), :])
                    zp, zm = z_up(*c), z_down(*c)
                    parts = []
                    for h in range(2):
                        near = (
                            (f[p + 1, h, rows(y), :], f[p - 1, h, rows(y), :]),
                            (f[p, h, rows(y, 1), :], f[p, h, rows(y, -1), :]),
                            (zp[h], zm[h]),
                        )
                        parts.append([(b - c[h], c[h] - a, b - a) for b, a in near])
                    both_.append(parts)
                for h in range(2):
                    (ux, uy, uz), (lx, ly, lz) = both_[0][h], both_[1][h]
                    m = [a[0] * b[0] + a[1] * b[1] for a, b in ((ux, lx), (uy, ly), (uz, lz))]
                    f_xx, f_xy, f_xz, f_yz, f_yy, f_zz = (fp[c, p, h, rows(y), :] for c in range(6))
                    cross = (
                        ux[2] * (f_xy * ly[2] + f_xz * lz[2])
                        + uy[2] * (f_xy * lx[2] + f_yz * lz[2])
                        + uz[2] * (f_xz * lx[2] + f_yz * ly[2])
                    )
                    total_l[h] = total_l[h] + ((m[0] * f_xx + m[1] * f_yy) + (m[2] * f_zz + 0.5 * cross))
                    total_t[h] = total_t[h] + (m[0] + m[1] + m[2])
            return (*total_l, *total_t)

        zero = jnp.zeros((8, ZL), jnp.float32)
        sums = lax.fori_loop(1, NX + 1, body, (zero,) * 4)
        for i in range(4):
            acc[i] = acc[i] + sums[i]

    def adjoint(n, k, put):
        def react(p, y, c):
            q = slice(y, y + 8)
            out = []
            for h in range(2):
                u = us[n][p, h, rows(y), :]
                w = ws[n][p - 1, h, q, :]
                m = mu[p - 1, h, q, :]
                rate = (1.0 - 8.0 * DT * 0.15) + u * (8.0 * DT * 2.3 - 24.0 * DT * u) - DT * w
                out.append(c[h] * rate - (16.0 * DT * EPS_W * u - 8.0 * DT * EPS_W * 1.15) * m)
                if n > 0:
                    mu[p - 1, h, q, :] = (1.0 - DT * EPS_W) * m - DT * u * c[h]
            return out

        apply(k, react, put)

    for n in range(STEPS - 1, 0, -1):
        k = 4 + STEPS - 1 - n
        wait_recv(exchange(k))
        install(k)
        adjoint(n, k, put_field(k + 1))
        start(exchange(k + 1))
        sens(n, k)
    wait_recv(exchange(7))
    install(7)
    sens(0, 7)

    scale = -0.5 * DT / TILE**1.5
    flat = []
    for h in range(2):
        s_l = jnp.broadcast_to(jnp.sum(acc[h], axis=0, keepdims=True), (8, ZL))
        s_a = jnp.broadcast_to(jnp.sum(acc[2 + h], axis=0, keepdims=True), (8, ZL))
        flat.append((scale * own_t[h] * s_l, scale * own_t[h] * (s_a - s_l)))

    def parts_of(group):
        ids = subf + (8 * group).astype(jnp.float32)
        tot = []
        for j in range(2):
            v = sum(jnp.where(own_r[h] == ids, flat[h][j], 0.0) for h in range(2))
            tot.append(v + pltpu.roll(v, 64, 1))
        return jnp.where(lanes < 64, tot[0], tot[1])

    rrecv[0] = parts_of(gx)

    def r1(k):
        return remote(rsend.at[k], rrecv.at[k], r1s, r1r, (lax.rem(gx + k, gx_count), gy))

    @pl.loop(1, gx_count)
    def _(k):
        rsend[k] = parts_of(lax.rem(gx + k, gx_count))
        r1(k).start()

    adjoint(0, 7, put_last(llast))
    for copy in store(llast, out_lam, 1):
        copy.start()

    remote(rsend.at[pl.ds(1, gx_count - 1)], rrecv.at[pl.ds(1, gx_count - 1)], r1s, r1r, (gx, gy)).wait_recv()
    total = lax.fori_loop(0, gx_count, lambda k, s: s + rrecv[k], jnp.zeros((8, ZL), jnp.float32))
    rg[0] = total

    def r2(k):
        return remote(rg.at[0], rg.at[k], r2s.at[k], r2r.at[k], (gx, lax.rem(gy + k, gy_count)))

    for k in range(1, gy_count):
        r2(k).start()
    for k in range(1, gy_count):
        r2(k).wait_recv()
        total = total + rg[k]
    for j in range(2):
        mine_row = sub == 2 * gy + j
        out_l[j] = jnp.sum(jnp.where(jnp.logical_and(mine_row, lanes < 64), total, 0.0))
        out_t[j] = jnp.sum(jnp.where(jnp.logical_and(mine_row, lanes >= 64), total, 0.0))

    wait_send(tile_copies())
    wait_send(fiber_exchange())
    for k in range(8):
        wait_send(exchange(k))
    for k in range(1, gy_count):
        g1(k).wait_send()
        r2(k).wait_send()
    remote(quad.at[pl.ds(1, gx_count - 1)], quad.at[pl.ds(1, gx_count - 1)], g2s, g2r, (gx, gy)).wait_send()
    remote(rsend.at[pl.ds(1, gx_count - 1)], rrecv.at[pl.ds(1, gx_count - 1)], r1s, r1r, (gx, gy)).wait_send()
    for copy in store(ulast, out_u, 0) + store(llast, out_lam, 1):
        copy.wait()


def solution(mesh):
    gx_count, gy_count = mesh.shape["gx"], mesh.shape["gy"]

    def local(*args):
        any_, smem = pl.BlockSpec(memory_space=pl.ANY), pl.BlockSpec(memory_space=pltpu.SMEM)
        f32 = jnp.float32
        padded = pltpu.VMEM((NX + 2, 2, YP, ZL), f32)
        plain = pltpu.VMEM((NX, 2, NY, ZL), f32)
        dma = pltpu.SemaphoreType.DMA
        scratch = [padded] * 8 + [plain] * 2 + [plain] * 4 + [plain]
        scratch += [
            pltpu.VMEM((6, NX + 2, 2, YP, ZL), f32),
            pltpu.VMEM((NX + 1, 2, NY, ZL), f32),
            pltpu.VMEM((NX + 1, 2, NY, ZL), f32),
            pltpu.VMEM((NX + 1, 2, NY, ZL), f32),
            pltpu.VMEM((NX + 1, NY, ZL), f32),
            pltpu.VMEM((3, NX + 2, 2, NY, ZL), f32),
            plain,
            padded,
            padded,
            padded,
            pltpu.VMEM((8, 2, 2, NX, ZL), f32),
            pltpu.VMEM((8, 2, 2, YP, ZL), f32),
            pltpu.VMEM((8, 4, 2, 8, ZL), f32),
            pltpu.VMEM((2, 3, 2, NX, ZL), f32),
            pltpu.VMEM((2, 3, 2, NX, ZL), f32),
            pltpu.VMEM((2, 2, 2, NX, ZL), f32),
            pltpu.VMEM((2, 2, NX, ZL), f32),
            pltpu.VMEM((2, 2, NX, ZL), f32),
            pltpu.VMEM((8, ZL), f32),
            pltpu.VMEM((4, 8, ZL), f32),
            pltpu.VMEM((8, ZL), f32),
            pltpu.VMEM((gy_count, 8, ZL), f32),
            pltpu.VMEM((gx_count, 8, ZL), f32),
            pltpu.VMEM((gx_count, 8, ZL), f32),
            pltpu.VMEM((gx_count, 8, ZL), f32),
            pltpu.VMEM((gy_count, 8, ZL), f32),
            pltpu.VMEM((5, 2, 2, 8, ZL), f32),
            pltpu.VMEM((4, 8, ZL), f32),
            dma((6, 2)),
            dma((8, 8)),
            dma((8, 8)),
            dma((4,)),
            dma((4,)),
            dma((4,)),
            dma((4,)),
            dma((gy_count,)),
            dma((gy_count,)),
            dma(()),
            dma(()),
            dma(()),
            dma(()),
            dma((gy_count,)),
            dma((gy_count,)),
        ]
        field = jax.ShapeDtypeStruct((NX, NY, 2 * ZL), f32)
        two = jax.ShapeDtypeStruct((2,), f32)

        def body(*refs):
            kernel(gx_count, gy_count, *refs)

        return pl.pallas_call(
            body,
            out_shape=(field, field, two, two),
            in_specs=[any_] * 5 + [smem] * 4,
            out_specs=(any_, any_, smem, smem),
            scratch_shapes=scratch,
            compiler_params=pltpu.CompilerParams(
                collective_id=0, has_side_effects=True, vmem_limit_bytes=60 * 1024 * 1024
            ),
        )(*args[:3], *args[7:], *args[3:7])

    return jax.shard_map(
        local,
        mesh=mesh,
        in_specs=(
            P("gx", "gy", None),
            P("gx", "gy", None),
            P(None, "gx", "gy", None),
            P(("gx", "gy")),
            P(("gx", "gy")),
            P("gx", "gy", None),
            P("gx", "gy", None),
            P("gx", "gy", None),
            P("gx", "gy", None),
        ),
        out_specs=(P("gx", "gy", None), P("gx", "gy", None), P(("gx", "gy")), P(("gx", "gy"))),
        check_vma=False,
    )
```

time: 600 us -> 117 us (0.20); the launches traced: 591 us -> 117 us
  other arithmetic: 261 us -> 0 us
  blocking collectives: 177 us -> 0 us
  starting transfers between devices: 114 us -> 0 us
  Pallas kernels: 0 us -> 112 us
  local copies, waits for them, and re-layouts: 27.5 us -> 4.4 us
  waiting for transfers between devices: 8.84 us -> 0 us
    unnamed x2 -> x0, blocking collectives: 177 us -> none
    ppermute x36 -> x0, starting transfers between devices: 114 us -> none  [the longest x18 84.2 us: padded_2(): before = lax.ppermute(last, axis, up)]
    pallas_call x0 -> x1, Pallas kernels: none -> 112 us  [local(): pl.pallas_call(body, out_shape=(field, field, two, two), in_specs=[any_]...]
    add x4 -> x0, other arithmetic: 94.4 us -> none  [local(): field + TIME_STEP * (lap + ionic)]
    reduce_sum x6 -> x0, other arithmetic: 49.7 us -> none  [the longest x4 48.7 us: tile_sums(): return field.reshape(sizes[0] // tile, tile, sizes[1] // tile, tile, size...]
    concatenate x15 -> x0, other arithmetic: 46.9 us -> none  [padded_2(): shard = jnp.concatenate([before, shard, after], axis=dim)]
    sub x4 -> x0, other arithmetic: 27.3 us -> none  [the longest x3 27.2 us: local(): adjoint + TIME_STEP * (lap + slope * adjoint)]
    unnamed x5 -> x0, other arithmetic: 23.8 us -> none
  transfers between devices with their start and end apart: 36 -> 0, of which waited for: 9 -> 0; matrix products, arithmetic and copies ran while one was open for 13% -> 0% of each run, Pallas kernels for 0% -> 0%
where the time goes in v1:
time: 117 us
  Pallas kernels  112 us (96%)
  local copies, waits for them, and re-layouts  4.4 us (4%)
    pallas_call x1, Pallas kernels, local(): pl.pallas_call(body, out_shape=(field, field, two, two), in_specs=[any_]...  112 us
    unnamed x10, local copies, waits for them, and re-layouts  4.4 us

profile of v1, /device:TPU:1, one launch (start us, length us, event | category | flops | bytes accessed | tf_op | source)
XLA Modules:
  0.0 116.6 jit_solution(3781982770535434021)
XLA Ops:
  0.6 111.6 %shard_map.120 = (f32[32,32,256]{2,1,0:T(8,128)}, f32[32,32,256]{2,1,0:T(8,128)}, f32[2]{0:T(128)}, f32[2]{0:T(128)}) custom-call(f32[32,32,256]{2,1,0:T(8,128)} %refs_0_.1, f32[32,32,256]{2,1,0:T(8,128)} %refs_1_.1, f32[2,32,32,256]{3,2,1,0:T(8,128)} %refs_2_.1, f32[32,32,256]{2,1,0:T(8,128)} %refs_3_.1, f32[32,32,256]{2,1,0:T(8,128)} %refs_4_.1, ...), custom_call_target="tpu_custom_call" | custom-call | tf_op jit(solution)/shard_map/pallas_call | solution.py:808
  112.2 0.0 copy-start
  112.2 0.0 copy-start.2
  112.2 0.0 copy-start.1
  112.2 2.4 %copy.17 = f32[32,32,256]{2,1,0:T(8,128)} copy(f32[32,32,256]{2,1,0:T(8,128)} %get-tuple-element.8) | data formatting | bytes 2097152
  114.6 0.0 copy-done
  114.6 1.0 copy.18
  115.6 0.0 copy-done.2
  115.6 0.5 copy.19
  116.1 0.0 copy-done.1
  116.1 0.5 copy.20
Async XLA Ops:
  112.2 2.4 %copy-start = (f32[32,32,256]{2,1,0:T(8,128)S(1)}, f32[32,32,256]{2,1,0:T(8,128)}, u32[]{:S(2)}) copy-start(f32[32,32,256]{2,1,0:T(8,128)} %get-tuple-element.9) | copy-start | bytes 3145732
  112.2 3.4 %copy-start.2 = (f32[2]{0:T(128)S(1)}, f32[2]{0:T(128)}, u32[]{:S(2)}) copy-start(f32[2]{0:T(128)} %get-tuple-element.10) | copy-start | bytes 28
  112.2 3.9 %copy-start.1 = (f32[2]{0:T(128)S(1)}, f32[2]{0:T(128)}, u32[]{:S(2)}) copy-start(f32[2]{0:T(128)} %get-tuple-element.11) | copy-start | bytes 28

commit v2 on v1

v2 whole, which is shorter than its diff:
```python
import jax
import jax.numpy as jnp
from jax import lax
from jax.experimental import pallas as pl
from jax.experimental.pallas import tpu as pltpu
from jax.sharding import PartitionSpec as P

MESH = pl.DeviceIdType.MESH
STEPS = 4
DT = 0.05
EPS_W = 0.1
NX, NY, ZL = 32, 32, 128
Y0 = 8
YP = 48
YT = NY // 8
TILE = 32

XX, XY, XZ, YZ, YY, ZZ = range(6)

SIN = (0.9999999954376937, -0.16666657521871267, 0.008333039791882324, -0.0001980823258586027, 2.603293610558432e-06)
COS = (
    0.9999999997626233,
    -0.4999999931520218,
    0.041666634639589036,
    -0.0013888340619260778,
    2.4759088421126325e-05,
    -2.6032335044441285e-07,
)


def poly(z, coefs):
    total = coefs[-1] * z + coefs[-2]
    for value in coefs[-3::-1]:
        total = total * z + value
    return total


def sincos(x):
    t = (1.5707963705062866 - jnp.abs(x)) - 4.371139000186241e-08
    z = t * t
    cosine = t * poly(z, SIN)
    size = poly(z, COS)
    return jnp.where(x < 0.0, -size, size), cosine


def products(theta, phi):
    st, ct = sincos(theta)
    sp, cp = sincos(phi)
    fx, fy, fz = cp * ct, cp * st, sp
    return {XX: fx * fx, YY: fy * fy, ZZ: fz * fz, XY: fx * fy, XZ: fx * fz, YZ: fy * fz}


def lane():
    return lax.broadcasted_iota(jnp.int32, (8, ZL), 1)


def z_up(h0, h1):
    last = lane() == ZL - 1
    r0, r1 = pltpu.roll(h0, ZL - 1, 1), pltpu.roll(h1, ZL - 1, 1)
    return jnp.where(last, r1, r0), jnp.where(last, 0.0, r1)


def z_down(h0, h1, edge=0.0):
    first = lane() == 0
    r0, r1 = pltpu.roll(h0, 1, 1), pltpu.roll(h1, 1, 1)
    return jnp.where(first, edge, r0), jnp.where(first, r0, r1)


def pair(fn):
    return fn(0), fn(1)


def kernel(
    gx_count,
    gy_count,
    pot,
    rec,
    fib,
    cot_p,
    cot_r,
    sig_l_in,
    sig_t_in,
    region_in,
    tissue_in,
    out_u,
    out_lam,
    out_l,
    out_t,
    u0,
    u1,
    u2,
    u3,
    l4,
    l3,
    l2,
    l1,
    ulast,
    llast,
    r0,
    r1_,
    r2_,
    r3,
    ww,
    mu,
    fp,
    dx,
    dy,
    dz,
    dzm,
    ex,
    fhx,
    fhy,
    tt,
    bb,
    py,
    ay,
    ysend,
    halo,
    crecv,
    fysend,
    frecv,
    cfd,
    cfh,
    cfo,
    tinfo,
    trecv,
    g1send,
    g1recv,
    quad,
    rsend,
    rrecv,
    rg,
    sv,
    acc,
    sig_l,
    sig_t,
    region,
    tissue,
    load_sem,
    small_sem,
    xs,
    xr,
    fs,
    fr,
    ts,
    tr,
    g1s,
    g1r,
    g2s,
    g2r,
    r1s,
    r1r,
    r2s,
    r2r,
):
    gx, gy = lax.axis_index("gx"), lax.axis_index("gy")
    has = {"l": gx > 0, "r": gx < gx_count - 1, "d": gy > 0, "u": gy < gy_count - 1}
    us = (u0, u1, u2, u3)
    ls = (l4, l3, l2, l1)
    rs = (r0, r1_, r2_, r3)
    fields = us + ls
    data = pl.ds(Y0, NY)
    names = "lrdu"
    corner_list = (("l", "d"), ("l", "u"), ("r", "d"), ("r", "u"))
    step_of = {"l": (-1, 0), "r": (1, 0), "d": (0, -1), "u": (0, 1)}

    def loads(index, src, dst, padded):
        out = []
        for h in range(2):
            s = src.at[:, :, pl.ds(h * ZL, ZL)]
            d = dst.at[pl.ds(1, NX), h, data, :] if padded else dst.at[:, h]
            out.append(pltpu.make_async_copy(s, d, load_sem.at[index, h]))
        return out

    copies = [
        loads(0, fib.at[0], tt, False),
        loads(1, fib.at[1], bb, True),
        loads(2, pot, u0, True),
        loads(3, cot_p, l4, True),
        loads(4, rec, ww, False),
        loads(5, cot_r, mu, False),
    ]
    small = [
        pltpu.make_async_copy(a, b, small_sem.at[i])
        for i, (a, b) in enumerate(((sig_l_in, sig_l), (sig_t_in, sig_t), (region_in, region), (tissue_in, tissue)))
    ]
    for copy in small:
        copy.start()
    for group in copies:
        for copy in group:
            copy.start()

    barrier = pltpu.get_barrier_semaphore()

    def both(a, b):
        return jnp.logical_and(has[a], has[b])

    def target(*sides):
        return (gx + sum(step_of[s][0] for s in sides), gy + sum(step_of[s][1] for s in sides))

    for a, b in corner_list:

        @pl.when(both(a, b))
        def _(a=a, b=b):
            pl.semaphore_signal(barrier, inc=1, device_id=target(a, b), device_id_type=MESH)

    @pl.loop(1, gy_count)
    def _(k):
        pl.semaphore_signal(barrier, inc=1, device_id=(gx, lax.rem(gy + k, gy_count)), device_id_type=MESH)

    @pl.loop(1, gx_count)
    def _(k):
        pl.semaphore_signal(barrier, inc=1, device_id=(lax.rem(gx + k, gx_count), gy), device_id_type=MESH)

    gxi = (gx > 0).astype(jnp.int32) + (gx < gx_count - 1).astype(jnp.int32)
    gyi = (gy > 0).astype(jnp.int32) + (gy < gy_count - 1).astype(jnp.int32)

    def remote(src, dst, send, recv, device):
        return pltpu.make_async_remote_copy(
            src_ref=src, dst_ref=dst, send_sem=send, recv_sem=recv, device_id=device, device_id_type=MESH
        )

    zero = jnp.zeros((8, ZL), jnp.float32)
    face0 = jnp.zeros((2, NY, ZL), jnp.float32)
    line0 = jnp.zeros((1, ZL), jnp.float32)
    for f in fields:
        f[0, :, Y0 : Y0 + NY, :] = face0
        f[NX + 1, :, Y0 : Y0 + NY, :] = face0
    bb[0, :, Y0 : Y0 + NY, :] = face0

    @pl.loop(1, NX + 1)
    def _(p):
        for h in range(2):
            for f in fields:
                f[p, h, Y0 - 1 : Y0, :] = line0
                f[p, h, Y0 + NY : Y0 + NY + 1, :] = line0
            ay[p, h, Y0 - 1 : Y0, :] = line0
            py[p, h, Y0 + NY : Y0 + NY + 1, :] = line0

    for i, name in enumerate(names):

        @pl.when(jnp.logical_not(has[name]))
        def _(i=i):
            for k in range(8):
                halo[k, i, :, Y0 : Y0 + NY, :] = face0
            for c in range(3):
                frecv[i, c] = face0
            trecv[i] = zero

    for c, (a, b) in enumerate(corner_list):

        @pl.when(jnp.logical_not(both(a, b)))
        def _(c=c):
            for k in range(8):
                crecv[k, c] = jnp.zeros((2, 8, ZL), jnp.float32)

    for i in range(4):
        for h in range(2):
            cfo[i, 0, h, Y0 - 1 : Y0, :] = line0
            cfo[i, 0, h, Y0 + NY : Y0 + NY + 1, :] = line0
    acc[...] = jnp.zeros_like(acc)

    for copy in small:
        copy.wait()
    lanes = lane()
    tile_of = lanes // TILE

    def lane_vector(ref, h):
        value = zero
        for k in range(4):
            value = jnp.where(tile_of == k, ref[0, 0, 4 * h + k].astype(jnp.float32), value)
        return value

    own_r = [lane_vector(region, h) for h in range(2)]
    own_t = [lane_vector(tissue, h) for h in range(2)]
    sub = lax.broadcasted_iota(jnp.int32, (8, ZL), 0)
    subf = sub.astype(jnp.float32)
    tinfo[...] = jnp.where(
        sub == 0, own_r[0], jnp.where(sub == 1, own_r[1], jnp.where(sub == 2, own_t[0], own_t[1]))
    )
    value = jnp.where(
        lanes < 64, jnp.where(sub == 2 * gy, sig_l[0], sig_l[1]), jnp.where(sub == 2 * gy, sig_t[0], sig_t[1])
    )
    mine = jnp.where(jnp.logical_or(sub == 2 * gy, sub == 2 * gy + 1), value, 0.0)
    g1send[...] = mine

    other = (1, 0, 3, 2)

    def start(list_):
        for cond, _, copy in list_:

            @pl.when(cond)
            def _(copy=copy):
                copy.start()

    def wait_recv(list_):
        for _, cond, copy in list_:

            @pl.when(cond)
            def _(copy=copy):
                copy.wait_recv()

    def wait_send(list_):
        for cond, _, copy in list_:

            @pl.when(cond)
            def _(copy=copy):
                copy.wait_send()

    def to_faces(sources, dest, send, recv):
        return [
            (has[s], has[names[other[i]]], remote(sources[i], dest(other[i]), send(i), recv(other[i]), target(s)))
            for i, s in enumerate(names)
        ]

    def tile_copies():
        return to_faces([tinfo] * 4, lambda i: trecv.at[i], lambda i: ts.at[i], lambda i: tr.at[i])

    def fiber_exchange():
        first = pl.ds(0, 3)
        sources = [fp.at[first, 1, :, data, :], fp.at[first, NX, :, data, :], fysend.at[0], fysend.at[1]]
        return to_faces(sources, lambda i: frecv.at[i], lambda i: fs.at[i], lambda i: fr.at[i])

    def exchange(k):
        f = fields[k]
        sources = [f.at[1, :, data, :], f.at[NX, :, data, :], ysend.at[k, 0, :, data, :], ysend.at[k, 1, :, data, :]]
        out = to_faces(
            sources, lambda i: halo.at[k, i, :, data, :], lambda i: xs.at[k, i], lambda i: xr.at[k, i]
        )
        for c, (a, b) in enumerate(corner_list):
            xrow = Y0 if a == "l" else Y0 + NX - 8
            src = ysend.at[k, 0 if b == "d" else 1, :, pl.ds(xrow, 8), :]
            copy = remote(src, crecv.at[k, 3 - c], xs.at[k, 4 + c], xr.at[k, 7 - c], target(a, b))
            out.append((both(a, b), both(*corner_list[3 - c]), copy))
        return out

    def g1(k):
        return remote(g1send, g1recv.at[k], g1s.at[k], g1r.at[k], (gx, lax.rem(gy + k, gy_count)))

    def g2(k):
        return remote(quad.at[0], quad.at[k], g2s, g2r, (lax.rem(gx + k, gx_count), gy))

    def wait_load(index):
        for copy in copies[index]:
            copy.wait()

    def pack_rows(f, k):
        @pl.loop(0, NX)
        def _(x):
            for h in range(2):
                ysend[k, 0, h, pl.ds(x + Y0, 1), :] = f[x + 1, h, Y0 : Y0 + 1, :]
                ysend[k, 1, h, pl.ds(x + Y0, 1), :] = f[x + 1, h, Y0 + NY - 1 : Y0 + NY, :]

    def trig(x):
        for yt in range(YT):
            y = yt * 8
            for h in range(2):
                got = products(tt[x, h, y : y + 8, :], bb[x + 1, h, Y0 + y : Y0 + y + 8, :])
                for c in range(6):
                    fp[c, x + 1, h, Y0 + y : Y0 + y + 8, :] = got[c]
                for i, c in enumerate((YY, XY, YZ)):
                    if yt == 0:
                        fysend[0, i, h, pl.ds(x, 1), :] = got[c][0:1]
                    if yt == YT - 1:
                        fysend[1, i, h, pl.ds(x, 1), :] = got[c][7:8]

    wait_load(0)
    wait_load(1)
    pl.loop(0, NX // 2)(trig)
    pl.semaphore_wait(barrier, gx_count - 1 + gy_count - 1 + gxi * gyi)
    for k in range(1, gy_count):
        g1(k).start()
    start(tile_copies())
    wait_load(2)
    pack_rows(u0, 0)
    start(exchange(0))
    pl.loop(NX // 2, 3 * NX // 4)(trig)
    quad_own = mine
    for k in range(1, gy_count):
        g1(k).wait_recv()
        quad_own = quad_own + g1recv[k]
    quad[0] = quad_own

    @pl.loop(1, gx_count)
    def _(k):
        g2(k).start()

    pl.loop(3 * NX // 4, NX)(trig)
    start(fiber_exchange())
    wait_load(3)
    pack_rows(l4, 4)
    start(exchange(4))

    wait_recv(tile_copies())
    remote(quad.at[pl.ds(1, gx_count - 1)], quad.at[pl.ds(1, gx_count - 1)], g2s, g2r, (gx, gy)).wait_recv()
    regions = list(own_r)
    flags = list(own_t)
    for i in range(4):
        for h in range(2):
            regions.append(jnp.broadcast_to(trecv[i, h : h + 1, :], (8, ZL)))
            flags.append(jnp.broadcast_to(trecv[i, 2 + h : 3 + h, :], (8, ZL)))

    def lookup(k, sums):
        tile = quad[k]
        turned = pltpu.roll(tile, 64, 1)
        low = lanes < 64
        long_, trans = jnp.where(low, tile, turned), jnp.where(low, turned, tile)
        group = lax.rem(gx - k + gx_count, gx_count)
        ids = subf + (8 * group).astype(jnp.float32)
        new = []
        for i in range(10):
            hit = regions[i] == ids
            new.append(jnp.where(hit, long_, sums[2 * i]))
            new.append(jnp.where(hit, trans, sums[2 * i + 1]))
        return tuple(new)

    sums = lax.fori_loop(0, gx_count, lookup, (zero,) * 20)
    for i in range(10):
        s_l = jnp.broadcast_to(jnp.sum(sums[2 * i], axis=0, keepdims=True), (8, ZL)) * flags[i]
        s_t = jnp.broadcast_to(jnp.sum(sums[2 * i + 1], axis=0, keepdims=True), (8, ZL)) * flags[i]
        sv[i // 2, 0, i % 2] = s_t
        sv[i // 2, 1, i % 2] = s_l - s_t

    c_pair = 0.25 * DT
    c_axis = 0.5 * DT
    st = pair(lambda h: sv[0, 0, h])
    ee = pair(lambda h: sv[0, 1, h])
    ea = pair(lambda h: c_axis * ee[h])
    ep = pair(lambda h: c_pair * ee[h])
    s2 = pair(lambda h: DT * st[h])

    def coefficients(p):
        for yt in range(YT):
            y = yt * 8
            r = slice(Y0 + y, Y0 + y + 8)
            q = slice(y, y + 8)
            dzz = []
            for h in range(2):
                sum_x = fp[XX, p, h, r, :] + fp[XX, p + 1, h, r, :]
                sum_y = fp[YY, p, h, r, :] + fp[YY, p, h, Y0 + y + 1 : Y0 + y + 9, :]
                if yt == YT - 1:
                    sum_y = jnp.where(sub == 7, 0.0, sum_y)
                fhx[p, h, q, :] = sum_x
                fhy[p, h, q, :] = sum_y
                dx[p, h, q, :] = s2[h] + ea[h] * sum_x
                dy[p, h, q, :] = s2[h] + ea[h] * sum_y
                dzz.append(c_axis * st[h] + ea[h] * fp[ZZ, p, h, r, :])
                for i, c in enumerate((XY, XZ, YZ)):
                    ex[i, p, h, q, :] = ep[h] * fp[c, p, h, r, :]
            up = z_up(*dzz)
            for h in range(2):
                dz[p, h, q, :] = dzz[h] + up[h]
            dzm[p, q, :] = dzz[0]

    pl.loop(1, NX + 1)(coefficients)
    wait_recv(fiber_exchange())

    def own_products(i, c, h, t):
        if i < 2:
            return fp[(XX, XY, XZ)[c], 1 if i == 0 else NX, h, Y0 + t * 8 : Y0 + t * 8 + 8, :]
        return fysend[i - 2, c, h, t * 8 : t * 8 + 8, :]

    for i in range(4):
        for h in range(2):
            st_n, e_n = sv[1 + i, 0, h], sv[1 + i, 1, h]
            for t in range(4):
                q = slice(t * 8, t * 8 + 8)
                total = (st_n + e_n * frecv[i, 0, h, q, :]) + (st[h] + ee[h] * own_products(i, 0, h, t))
                cfd[i, h, q, :] = c_axis * total
                if i == 1:
                    dx[NX, h, q, :] = c_axis * total
                    fhx[NX, h, q, :] = zero
                for j in range(2):
                    cfh[i, j, h, q, :] = c_pair * e_n * frecv[i, 1 + j, h, q, :]
                    cfo[i, j, h, Y0 + t * 8 : Y0 + t * 8 + 8, :] = ep[h] * own_products(i, 1 + j, h, t)

    for x in range(NX):
        for h in range(2):
            dy[x + 1, h, NY - 1 : NY, :] = cfd[3, h, x : x + 1, :]

    def rows(y, shift=0):
        return slice(Y0 + y + shift, Y0 + y + shift + 8)

    def near(f, p, y):
        c = pair(lambda h: f[p, h, rows(y), :])
        xp = pair(lambda h: f[p + 1, h, rows(y), :])
        xm = pair(lambda h: f[p - 1, h, rows(y), :])
        yp = pair(lambda h: f[p, h, rows(y, 1), :])
        ym = pair(lambda h: f[p, h, rows(y, -1), :])
        return c, xp, xm, yp, ym, z_up(*c), z_down(*c)

    def stage_a(f, p, yt, react, sens=None):
        y = yt * 8
        q = slice(y, y + 8)
        c, xp, xm, yp, ym, zp, zm = near(f, p, y)
        own = react(p, y, c)
        if sens is not None:
            u, sums = sens
            v, vxp, vxm, vyp, vym, vzp, vzm = near(u, p, y)
        flux_x, local, pz, az, prod_z = [], [], [], [], []
        for h in range(2):
            g_x, g_y, g_z = xp[h] - xm[h], yp[h] - ym[h], zp[h] - zm[h]
            if sens is None:
                e_xy, e_xz, e_yz = (ex[i, p, h, q, :] for i in range(3))
            else:
                e_xy, e_xz, e_yz = (fp[i, p, h, rows(y), :] for i in (XY, XZ, YZ))
            p_x = e_xy * g_y + e_xz * g_z
            p_y = e_xy * g_x + e_yz * g_z
            p_z = e_xz * g_x + e_yz * g_y
            d_x, d_y, d_z = xp[h] - c[h], yp[h] - c[h], zp[h] - c[h]
            if sens is not None:
                cross = (vxp[h] - vxm[h]) * p_x + (vyp[h] - vym[h]) * p_y + (vzp[h] - vzm[h]) * p_z
                m_x, m_y, m_z = d_x * (vxp[h] - v[h]), d_y * (vyp[h] - v[h]), d_z * (vzp[h] - v[h])
                sums[h] = sums[h] + ((fhx[p, h, q, :] * m_x + fhy[p, h, q, :] * m_y) + 0.5 * cross)
                sums[2 + h] = sums[2 + h] + (m_x + m_y)
                prod_z.append(m_z)
                p_x, p_y, p_z = ep[h] * p_x, ep[h] * p_y, ep[h] * p_z
            f_x = dx[p, h, q, :] * d_x
            f_y = dy[p, h, q, :] * d_y
            f_z = dz[p, h, q, :] * d_z
            back = bb[p - 1, h, rows(y), :]
            bb[p, h, rows(y), :] = f_x + p_x
            py[p, h, rows(y), :] = p_y
            ay[p, h, rows(y), :] = f_y + p_y
            pz.append(p_z)
            az.append(f_z + p_z)
            flux_x.append(p_x)
            local.append((own[h] + f_x) + (f_y - back))
            local[h] = local[h] + f_z
        up = z_up(*pz)
        down = z_down(*az, edge=dzm[p, q, :] * c[0])
        for h in range(2):
            tt[p - 1, h, q, :] = local[h] + (up[h] - down[h])
        if sens is not None:
            below = z_down(*prod_z, edge=c[0] * v[0])
            for h in range(2):
                m = prod_z[h] + below[h]
                sums[h] = sums[h] + fp[ZZ, p, h, rows(y), :] * m
                sums[4 + h] = sums[4 + h] + m
        return flux_x

    def stage_b(p, yt, flux_x, put):
        y = yt * 8
        for h in range(2):
            value = tt[p - 1, h, y : y + 8, :] + (py[p, h, rows(y, 1), :] - ay[p, h, rows(y, -1), :])
            put(p, h, yt, value if flux_x is None else value + flux_x[h])

    def apply(k, react, put, u=None):
        f = fields[k]
        sums = [zero] * 6

        def stage(p, yt, running):
            return stage_a(f, p, yt, react, None if u is None else (u, running))

        for yt in range(YT):
            stage(1, yt, sums)

        def body(p, carry):
            running = list(carry)
            for yt in range(YT):
                stage_b(p - 1, yt, stage(p, yt, running), put)
            return tuple(running)

        if u is None:
            lax.fori_loop(2, NX + 1, lambda p, carry: (body(p, [zero] * 6), carry)[1], 0)
        else:
            sums = lax.fori_loop(2, NX + 1, body, tuple(sums))
            for h in range(2):
                acc[h] = acc[h] + sums[h]
                acc[2 + h] = acc[2 + h] + (2.0 * sums[2 + h] + sums[4 + h])
        for yt in range(YT):
            stage_b(NX, yt, None, put)

    def put_to(ref, slot, plane0, row0):
        def put(p, h, yt, value):
            ref[p - 1 + plane0, h, row0 + yt * 8 : row0 + yt * 8 + 8, :] = value
            if yt == 0:
                ysend[slot, 0, h, pl.ds(p - 1 + Y0, 1), :] = value[0:1]
            if yt == YT - 1:
                ysend[slot, 1, h, pl.ds(p - 1 + Y0, 1), :] = value[7:8]

        return put

    def install(k):
        for c, (a, b) in enumerate(corner_list):
            at = 7 if a == "l" else 0
            for h in range(2):
                v = crecv[k, c, h, at : at + 1, :]
                row = Y0 - 1 if b == "d" else Y0 + NY
                halo[k, names.index(a), h, row : row + 1, :] = v
                row = Y0 - 1 if a == "l" else Y0 + NX
                halo[k, names.index(b), h, row : row + 1, :] = v
        for s in range(2):
            row = Y0 if s == 0 else Y0 + NY - 1
            for h in range(2):
                ysend[k, s, h, Y0 - 1 : Y0, :] = halo[k, 0, h, row : row + 1, :]
                ysend[k, s, h, Y0 + NX : Y0 + NX + 1, :] = halo[k, 1, h, row : row + 1, :]

    def layer(k, i, h, r):
        if i < 2:
            return fields[k][1 if i == 0 else NX, h, r, :]
        return ysend[k, i - 2, h, r, :]

    def delta(k, i, t):
        lo = i in (0, 2)
        y = t * 8
        q = slice(y, y + 8)
        c = pair(lambda h: halo[k, i, h, rows(y), :])
        zp, zm = z_up(*c), z_down(*c)
        turn = pair(lambda h: cfo[i, 1, h, rows(y), :] * c[h])
        tp, tm = z_up(*turn), z_down(*turn)
        out = []
        for h in range(2):
            bp, bm = halo[k, i, h, rows(y, 1), :], halo[k, i, h, rows(y, -1), :]
            total = cfh[i, 0, h, q, :] * (bp - bm) + cfh[i, 1, h, q, :] * (zp[h] - zm[h])
            total = total + (cfo[i, 0, h, rows(y, 1), :] * bp - cfo[i, 0, h, rows(y, -1), :] * bm)
            total = total + (tp[h] - tm[h])
            if lo:
                out.append(cfd[i, h, q, :] * (c[h] - layer(k, i, h, rows(y))) - total)
            else:
                out.append(cfd[i, h, q, :] * c[h] + total)
        return out

    def finish(k, ref, slot, plane0, row0):
        wait_recv(exchange(k))
        install(k)
        for i, plane in ((0, plane0), (1, plane0 + NX - 1)):
            for t in range(4):
                d = delta(k, i, t)
                for h in range(2):
                    r = slice(row0 + t * 8, row0 + t * 8 + 8)
                    ref[plane, h, r, :] = ref[plane, h, r, :] + d[h]
            x = Y0 if i == 0 else Y0 + NX - 1
            for h in range(2):
                ysend[slot, 0, h, x : x + 1, :] = ref[plane, h, row0 : row0 + 1, :]
                ysend[slot, 1, h, x : x + 1, :] = ref[plane, h, row0 + NY - 1 : row0 + NY, :]
        for i in (2, 3):
            for t in range(4):
                d = delta(k, i, t)
                for h in range(2):
                    ysend[slot, i - 2, h, rows(t * 8), :] = ysend[slot, i - 2, h, rows(t * 8), :] + d[h]
        for x in (0, NX - 1):
            write_back(x, ref, slot, plane0, row0)

    def write_back(x, ref, slot, plane0, row0):
        for h in range(2):
            ref[x + plane0, h, row0 : row0 + 1, :] = ysend[slot, 0, h, x + Y0 : x + Y0 + 1, :]
            ref[x + plane0, h, row0 + NY - 1 : row0 + NY, :] = ysend[slot, 1, h, x + Y0 : x + Y0 + 1, :]

    def write_back_rest(ref, slot, plane0, row0):
        for x in range(1, NX - 1):
            write_back(x, ref, slot, plane0, row0)

    def store(ref, out, index):
        return [
            pltpu.make_async_copy(ref.at[:, h], out.at[:, :, pl.ds(h * ZL, ZL)], load_sem.at[index, h]) for h in range(2)
        ]

    wait_load(4)
    wait_load(5)
    for n in range(STEPS):

        def react(p, y, c, n=n):
            q = slice(y, y + 8)
            out = []
            for h in range(2):
                w = ww[p - 1, h, q, :]
                u = c[h]
                part = (8.0 * DT) * u
                turn = 8.0 * DT * 1.15 - part
                poly_ = u * turn
                rate = ((1.0 - 8.0 * DT * 0.15) - DT * w) + poly_
                out.append(u * rate)
                rs[n][p - 1, h, q, :] = rate + u * (turn - part)
                if n < STEPS - 1:
                    ww[p - 1, h, q, :] = (1.0 - DT * EPS_W) * w + EPS_W * poly_
            return out

        if n < STEPS - 1:
            place = (fields[n + 1], n + 1, 1, Y0)
        else:
            place = (ulast, 8, 0, 0)
        apply(n, react, put_to(*place))
        finish(n, *place)
        if n < STEPS - 1:
            start(exchange(n + 1))
        write_back_rest(*place)
    for copy in store(ulast, out_u, 0):
        copy.start()

    c_mu = 16.0 * DT * EPS_W

    def face_sums(n, k):
        sums = [zero] * 4
        for i in range(4):
            lo = i in (0, 2)
            for t in range(4):
                y = t * 8
                for_z = [pair(lambda h: layer(f, i, h, rows(y))) for f in (n, k)]
                zs = [(z_up(*c), z_down(*c)) for c in for_z]
                for h in range(2):
                    f_aa, f_ab, f_az = (own_products(i, c, h, t) for c in range(3))
                    flux = [
                        f_ab * (layer(f, i, h, rows(y, 1)) - layer(f, i, h, rows(y, -1))) + f_az * (z[0][h] - z[1][h])
                        for f, z in zip((n, k), zs)
                    ]
                    h_u, h_l = halo[n, i, h, rows(y), :], halo[k, i, h, rows(y), :]
                    o_u, o_l = for_z[0][h], for_z[1][h]
                    m = (o_u - h_u) * (o_l - h_l)
                    cross = 0.5 * (h_u * flux[1] + h_l * flux[0])
                    sums[h] = sums[h] + (f_aa * m - cross if lo else f_aa * m + cross)
                    sums[2 + h] = sums[2 + h] + (m if lo else m - 2.0 * (o_u * o_l))
        for i in range(4):
            acc[i] = acc[i] + sums[i]

    for n in range(STEPS - 1, -1, -1):
        k = 4 + STEPS - 1 - n

        def react(p, y, c, n=n):
            q = slice(y, y + 8)
            out = []
            for h in range(2):
                u = us[n][p, h, rows(y), :]
                m = mu[p - 1, h, q, :]
                if n == STEPS - 1:
                    m = c_mu * m
                out.append(c[h] * rs[n][p - 1, h, q, :] - (u - 0.575) * m)
                if n > 0:
                    mu[p - 1, h, q, :] = (1.0 - DT * EPS_W) * m - ((DT * c_mu) * c[h]) * u
            return out

        place = (fields[k + 1], k + 1, 1, Y0) if n > 0 else (llast, 9, 0, 0)
        apply(k, react, put_to(*place), us[n])
        finish(k, *place)
        if n > 0:
            start(exchange(k + 1))
        write_back_rest(*place)
        face_sums(n, k)
    for copy in store(llast, out_lam, 1):
        copy.start()

    scale = -0.5 * DT / TILE**1.5
    flat = []
    for h in range(2):
        s_l = jnp.broadcast_to(jnp.sum(acc[h], axis=0, keepdims=True), (8, ZL))
        s_a = jnp.broadcast_to(jnp.sum(acc[2 + h], axis=0, keepdims=True), (8, ZL))
        flat.append((scale * own_t[h] * s_l, scale * own_t[h] * (s_a - s_l)))

    def parts_of(group):
        ids = subf + (8 * group).astype(jnp.float32)
        tot = []
        for j in range(2):
            v = sum(jnp.where(own_r[h] == ids, flat[h][j], 0.0) for h in range(2))
            tot.append(v + pltpu.roll(v, 64, 1))
        return jnp.where(lanes < 64, tot[0], tot[1])

    rrecv[0] = parts_of(gx)

    def r1(k):
        return remote(rsend.at[k], rrecv.at[k], r1s, r1r, (lax.rem(gx + k, gx_count), gy))

    @pl.loop(1, gx_count)
    def _(k):
        rsend[k] = parts_of(lax.rem(gx + k, gx_count))
        r1(k).start()

    wait_send(tile_copies())
    wait_send(fiber_exchange())
    for k in range(8):
        wait_send(exchange(k))
    for k in range(1, gy_count):
        g1(k).wait_send()
    remote(quad.at[pl.ds(1, gx_count - 1)], quad.at[pl.ds(1, gx_count - 1)], g2s, g2r, (gx, gy)).wait_send()

    remote(rsend.at[pl.ds(1, gx_count - 1)], rrecv.at[pl.ds(1, gx_count - 1)], r1s, r1r, (gx, gy)).wait_recv()
    total = lax.fori_loop(0, gx_count, lambda k, s: s + rrecv[k], zero)
    rg[0] = total

    def r2(k):
        return remote(rg.at[0], rg.at[k], r2s.at[k], r2r.at[k], (gx, lax.rem(gy + k, gy_count)))

    for k in range(1, gy_count):
        r2(k).start()
    for k in range(1, gy_count):
        r2(k).wait_recv()
        total = total + rg[k]
    for j in range(2):
        mine_row = sub == 2 * gy + j
        out_l[j] = jnp.sum(jnp.where(jnp.logical_and(mine_row, lanes < 64), total, 0.0))
        out_t[j] = jnp.sum(jnp.where(jnp.logical_and(mine_row, lanes >= 64), total, 0.0))
    for k in range(1, gy_count):
        r2(k).wait_send()
    remote(rsend.at[pl.ds(1, gx_count - 1)], rrecv.at[pl.ds(1, gx_count - 1)], r1s, r1r, (gx, gy)).wait_send()
    for copy in store(ulast, out_u, 0) + store(llast, out_lam, 1):
        copy.wait()


def hand_on(u, lam, g_l, g_t, out_u, out_lam, out_l, out_t):
    out_u[...] = u[...]
    out_lam[...] = lam[...]
    for j in range(2):
        out_l[j] = g_l[j]
        out_t[j] = g_t[j]


def solution(mesh):
    gx_count, gy_count = mesh.shape["gx"], mesh.shape["gy"]

    def local(*args):
        any_, smem = pl.BlockSpec(memory_space=pl.ANY), pl.BlockSpec(memory_space=pltpu.SMEM)
        f32 = jnp.float32
        padded = pltpu.VMEM((NX + 2, 2, YP, ZL), f32)
        plain = pltpu.VMEM((NX, 2, NY, ZL), f32)
        dma = pltpu.SemaphoreType.DMA
        def vmem(*shape):
            return pltpu.VMEM(shape, f32)

        scratch = [padded] * 8 + [plain] * 2 + [plain] * 4 + [plain] * 2
        scratch += [
            vmem(6, NX + 2, 2, YP, ZL),
            vmem(NX + 1, 2, NY, ZL),
            vmem(NX + 1, 2, NY, ZL),
            vmem(NX + 1, 2, NY, ZL),
            vmem(NX + 1, NY, ZL),
            vmem(3, NX + 1, 2, NY, ZL),
            vmem(NX + 1, 2, NY, ZL),
            vmem(NX + 1, 2, NY, ZL),
            plain,
            padded,
            padded,
            padded,
            vmem(10, 2, 2, YP, ZL),
            vmem(8, 4, 2, YP, ZL),
            vmem(8, 4, 2, 8, ZL),
            vmem(2, 3, 2, NX, ZL),
            vmem(4, 3, 2, NX, ZL),
            vmem(4, 2, NX, ZL),
            vmem(4, 2, 2, NX, ZL),
            vmem(4, 2, 2, YP, ZL),
            vmem(8, ZL),
            vmem(4, 8, ZL),
            vmem(8, ZL),
            vmem(gy_count, 8, ZL),
            vmem(gx_count, 8, ZL),
            vmem(gx_count, 8, ZL),
            vmem(gx_count, 8, ZL),
            vmem(gy_count, 8, ZL),
            vmem(5, 2, 2, 8, ZL),
            vmem(4, 8, ZL),
            pltpu.SMEM((2,), f32),
            pltpu.SMEM((2,), f32),
            pltpu.SMEM((1, 1, 8), jnp.int32),
            pltpu.SMEM((1, 1, 8), jnp.int32),
            dma((6, 2)),
            dma((4,)),
            dma((8, 8)),
            dma((8, 8)),
            dma((4,)),
            dma((4,)),
            dma((4,)),
            dma((4,)),
            dma((gy_count,)),
            dma((gy_count,)),
            dma(()),
            dma(()),
            dma(()),
            dma(()),
            dma((gy_count,)),
            dma((gy_count,)),
        ]
        field = jax.ShapeDtypeStruct((NX, NY, 2 * ZL), f32)
        two = jax.ShapeDtypeStruct((2,), f32)

        def body(*refs):
            kernel(gx_count, gy_count, *refs)

        block = pl.BlockSpec((NX // 4, NY, 2 * ZL), lambda i: (i, 0, 0))
        made = pl.pallas_call(
            body,
            out_shape=(field, field, two, two),
            in_specs=[any_] * 9,
            out_specs=(any_, any_, smem, smem),
            scratch_shapes=scratch,
            compiler_params=pltpu.CompilerParams(
                collective_id=0, has_side_effects=True, vmem_limit_bytes=60 * 1024 * 1024
            ),
        )(*args[:3], *args[7:], *args[3:7])
        return pl.pallas_call(
            hand_on,
            grid=(4,),
            out_shape=(field, field, two, two),
            in_specs=[block, block, smem, smem],
            out_specs=(block, block, smem, smem),
        )(*made)

    return jax.shard_map(
        local,
        mesh=mesh,
        in_specs=(
            P("gx", "gy", None),
            P("gx", "gy", None),
            P(None, "gx", "gy", None),
            P(("gx", "gy")),
            P(("gx", "gy")),
            P("gx", "gy", None),
            P("gx", "gy", None),
            P("gx", "gy", None),
            P("gx", "gy", None),
        ),
        out_specs=(P("gx", "gy", None), P("gx", "gy", None), P(("gx", "gy")), P(("gx", "gy"))),
        check_vma=False,
    )
```

time: 117 us -> 88.5 us (0.76)
  Pallas kernels: 112 us -> 87.7 us
  local copies, waits for them, and re-layouts: 4.4 us -> 0 us
    pallas_call x1, Pallas kernels: 112 us -> 83.9 us  [local(): pl.pallas_call(body, out_shape=(field, field, two, two), in_specs=[any_]...]
    unnamed x10 -> x0, local copies, waits for them, and re-layouts: 4.4 us -> none
    pallas_call x0 -> x1, Pallas kernels: none -> 3.78 us  [local(): pl.pallas_call(hand_on, grid=(4,), out_shape=(field, field, two, two), in...]
where the time goes in v2:
time: 88.5 us; the launch traced here: 88.3 us
  Pallas kernels  87.7 us (99%)
    pallas_call x1, Pallas kernels, local(): pl.pallas_call(body, out_shape=(field, field, two, two), in_specs=[any_]...  83.9 us
    pallas_call x1, Pallas kernels, local(): pl.pallas_call(hand_on, grid=(4,), out_shape=(field, field, two, two), in...  3.78 us

profile of v2, /device:TPU:1, one launch (start us, length us, event | category | flops | bytes accessed | tf_op | source)
XLA Modules:
  0.0 88.3 jit_solution(15348413784619338533)
XLA Ops:
  0.6 83.9 %shard_map.120 = (f32[32,32,256]{2,1,0:T(8,128)}, f32[32,32,256]{2,1,0:T(8,128)}, f32[2]{0:T(128)}, f32[2]{0:T(128)}) custom-call(f32[32,32,256]{2,1,0:T(8,128)} %refs_0_.1, f32[32,32,256]{2,1,0:T(8,128)} %refs_1_.1, f32[2,32,32,256]{3,2,1,0:T(8,128)} %refs_2_.1, f32[32,32,256]{2,1,0:T(8,128)} %refs_3_.1, f32[32,32,256]{2,1,0:T(8,128)} %refs_4_.1, ...), custom_call_target="tpu_custom_call" | custom-call | tf_op jit(solution)/shard_map/pallas_call | solution.py:878
  84.6 3.8 %shard_map.121 = (f32[32,32,256]{2,1,0:T(8,128)}, f32[32,32,256]{2,1,0:T(8,128)}, f32[2]{0:T(128)}, f32[2]{0:T(128)}) custom-call(f32[32,32,256]{2,1,0:T(8,128)} %get-tuple-element.8.u, f32[32,32,256]{2,1,0:T(8,128)} %get-tuple-element.9.lam, f32[2]{0:T(128)} %get-tuple-element.10.g_l, f32[2]{0:T(128)} %get-tuple-element.11.g_t), custom_call_target="tpu_custom_call" | custom-call | tf_op jit(solution)/shard_map/pallas_call | solution.py:888

commit v3 on v2

--- a/solution.py
+++ b/solution.py
@@ -82,8 +82,8 @@
     sig_t_in,
     region_in,
     tissue_in,
-    out_u,
-    out_lam,
+    ulast,
+    llast,
     out_l,
     out_t,
     u0,
@@ -94,8 +94,6 @@
     l3,
     l2,
     l1,
-    ulast,
-    llast,
     r0,
     r1_,
     r2_,
@@ -114,6 +112,9 @@
     bb,
     py,
     ay,
+    px,
+    gzs,
+    dzs,
     ysend,
     halo,
     crecv,
@@ -366,15 +367,14 @@
 
     wait_load(0)
     wait_load(1)
-    pl.loop(0, NX // 2)(trig)
+    pl.loop(0, 2)(lambda i: trig(i * (NX - 1)))
+    pl.loop(1, 8)(trig)
     pl.semaphore_wait(barrier, gx_count - 1 + gy_count - 1 + gxi * gyi)
     for k in range(1, gy_count):
         g1(k).start()
     start(tile_copies())
-    wait_load(2)
-    pack_rows(u0, 0)
-    start(exchange(0))
-    pl.loop(NX // 2, 3 * NX // 4)(trig)
+    start(fiber_exchange()[:2])
+    pl.loop(8, 20)(trig)
     quad_own = mine
     for k in range(1, gy_count):
         g1(k).wait_recv()
@@ -385,11 +385,13 @@
     def _(k):
         g2(k).start()
 
-    pl.loop(3 * NX // 4, NX)(trig)
-    start(fiber_exchange())
+    pl.loop(20, NX - 1)(trig)
+    start(fiber_exchange()[2:])
+    wait_load(2)
+    pack_rows(u0, 0)
+    start(exchange(0))
     wait_load(3)
     pack_rows(l4, 4)
-    start(exchange(4))
 
     wait_recv(tile_copies())
     remote(quad.at[pl.ds(1, gx_count - 1)], quad.at[pl.ds(1, gx_count - 1)], g2s, g2r, (gx, gy)).wait_recv()
@@ -451,6 +453,9 @@
             for h in range(2):
                 dz[p, h, q, :] = dzz[h] + up[h]
             dzm[p, q, :] = dzz[0]
+            above = z_up(*pair(lambda h: fp[ZZ, p, h, r, :]))
+            for h in range(2):
+                fp[YY, p, h, r, :] = above[h]
 
     pl.loop(1, NX + 1)(coefficients)
     wait_recv(fiber_exchange())
@@ -481,23 +486,24 @@
     def rows(y, shift=0):
         return slice(Y0 + y + shift, Y0 + y + shift + 8)
 
-    def near(f, p, y):
+    def near(f, p, y, along_z=True):
         c = pair(lambda h: f[p, h, rows(y), :])
         xp = pair(lambda h: f[p + 1, h, rows(y), :])
         xm = pair(lambda h: f[p - 1, h, rows(y), :])
         yp = pair(lambda h: f[p, h, rows(y, 1), :])
         ym = pair(lambda h: f[p, h, rows(y, -1), :])
-        return c, xp, xm, yp, ym, z_up(*c), z_down(*c)
-
-    def stage_a(f, p, yt, react, sens=None):
+        around = (c, xp, xm, yp, ym)
+        return (*around, z_up(*c), z_down(*c)) if along_z else around
+
+    def stage_a(f, p, yt, react, backs, n, sens=None):
         y = yt * 8
         q = slice(y, y + 8)
         c, xp, xm, yp, ym, zp, zm = near(f, p, y)
         own = react(p, y, c)
         if sens is not None:
             u, sums = sens
-            v, vxp, vxm, vyp, vym, vzp, vzm = near(u, p, y)
-        flux_x, local, pz, az, prod_z = [], [], [], [], []
+            v, vxp, vxm, vyp, vym = near(u, p, y, False)
+        local, pz, az = [], [], []
         for h in range(2):
             g_x, g_y, g_z = xp[h] - xm[h], yp[h] - ym[h], zp[h] - zm[h]
             if sens is None:
@@ -508,68 +514,75 @@
             p_y = e_xy * g_x + e_yz * g_z
             p_z = e_xz * g_x + e_yz * g_y
             d_x, d_y, d_z = xp[h] - c[h], yp[h] - c[h], zp[h] - c[h]
-            if sens is not None:
-                cross = (vxp[h] - vxm[h]) * p_x + (vyp[h] - vym[h]) * p_y + (vzp[h] - vzm[h]) * p_z
-                m_x, m_y, m_z = d_x * (vxp[h] - v[h]), d_y * (vyp[h] - v[h]), d_z * (vzp[h] - v[h])
-                sums[h] = sums[h] + ((fhx[p, h, q, :] * m_x + fhy[p, h, q, :] * m_y) + 0.5 * cross)
+            if sens is None:
+                gzs[n, p - 1, h, q, :] = g_z
+                dzs[n, p - 1, h, q, :] = d_z
+            else:
+                cross = (vxp[h] - vxm[h]) * p_x + (vyp[h] - vym[h]) * p_y + gzs[n, p - 1, h, q, :] * p_z
+                m_x, m_y, m_z = d_x * (vxp[h] - v[h]), d_y * (vyp[h] - v[h]), d_z * dzs[n, p - 1, h, q, :]
+                sums[h] = sums[h] + (
+                    (fhx[p, h, q, :] * m_x + fhy[p, h, q, :] * m_y) + (fp[ZZ, p, h, rows(y), :] * m_z + 0.5 * cross)
+                )
                 sums[2 + h] = sums[2 + h] + (m_x + m_y)
-                prod_z.append(m_z)
+                sums[4 + h] = sums[4 + h] + m_z
+                sums[6 + h] = sums[6 + h] + fp[YY, p, h, rows(y), :] * m_z
+                if h == 0:
+                    m_0 = c[0] * v[0]
+                    sums[8] = sums[8] + fp[ZZ, p, 0, rows(y), :] * m_0
+                    sums[9] = sums[9] + m_0
                 p_x, p_y, p_z = ep[h] * p_x, ep[h] * p_y, ep[h] * p_z
             f_x = dx[p, h, q, :] * d_x
             f_y = dy[p, h, q, :] * d_y
             f_z = dz[p, h, q, :] * d_z
-            back = bb[p - 1, h, rows(y), :]
+            back = backs[yt][h]
             bb[p, h, rows(y), :] = f_x + p_x
             py[p, h, rows(y), :] = p_y
             ay[p, h, rows(y), :] = f_y + p_y
             pz.append(p_z)
             az.append(f_z + p_z)
-            flux_x.append(p_x)
+            px[p, h, q, :] = p_x
             local.append((own[h] + f_x) + (f_y - back))
             local[h] = local[h] + f_z
         up = z_up(*pz)
         down = z_down(*az, edge=dzm[p, q, :] * c[0])
         for h in range(2):
             tt[p - 1, h, q, :] = local[h] + (up[h] - down[h])
-        if sens is not None:
-            below = z_down(*prod_z, edge=c[0] * v[0])
-            for h in range(2):
-                m = prod_z[h] + below[h]
-                sums[h] = sums[h] + fp[ZZ, p, h, rows(y), :] * m
-                sums[4 + h] = sums[4 + h] + m
-        return flux_x
-
-    def stage_b(p, yt, flux_x, put):
+
+    def stage_b(p, yt, put, last=False):
         y = yt * 8
         for h in range(2):
             value = tt[p - 1, h, y : y + 8, :] + (py[p, h, rows(y, 1), :] - ay[p, h, rows(y, -1), :])
-            put(p, h, yt, value if flux_x is None else value + flux_x[h])
-
-    def apply(k, react, put, u=None):
+            put(p, h, yt, value if last else value + px[p + 1, h, y : y + 8, :])
+
+    def apply(k, n, react, put, u=None):
         f = fields[k]
-        sums = [zero] * 6
-
-        def stage(p, yt, running):
-            return stage_a(f, p, yt, react, None if u is None else (u, running))
-
+
+        def plane(p, running):
+            backs = [pair(lambda h: bb[p - 1, h, rows(yt * 8), :]) for yt in range(YT)]
+            for yt in range(YT):
+                stage_a(f, p, yt, react, backs, n, None if u is None else (u, running))
+
+        def body(p, carry, complete=True):
+            running = list(carry)
+            if complete:
+                for yt in range(YT):
+                    stage_b(p - 2, yt, put)
+            plane(p, running)
+            return tuple(running)
+
+        sums = (zero,) * (0 if u is None else 10)
+        sums = lax.fori_loop(1, 3, lambda p, carry: body(p, carry, False), sums)
+        sums = lax.fori_loop(3, NX + 1, body, sums)
+        if u is not None:
+            over_l = z_down(sums[6], sums[7], edge=sums[8])
+            over_t = z_down(sums[4], sums[5], edge=sums[9])
+            for h in range(2):
+                acc[h] = acc[h] + (sums[h] + over_l[h])
+                acc[2 + h] = acc[2 + h] + (2.0 * sums[2 + h] + (sums[4 + h] + over_t[h]))
         for yt in range(YT):
-            stage(1, yt, sums)
-
-        def body(p, carry):
-            running = list(carry)
-            for yt in range(YT):
-                stage_b(p - 1, yt, stage(p, yt, running), put)
-            return tuple(running)
-
-        if u is None:
-            lax.fori_loop(2, NX + 1, lambda p, carry: (body(p, [zero] * 6), carry)[1], 0)
-        else:
-            sums = lax.fori_loop(2, NX + 1, body, tuple(sums))
-            for h in range(2):
-                acc[h] = acc[h] + sums[h]
-                acc[2 + h] = acc[2 + h] + (2.0 * sums[2 + h] + sums[4 + h])
+            stage_b(NX - 1, yt, put)
         for yt in range(YT):
-            stage_b(NX, yt, None, put)
+            stage_b(NX, yt, put, True)
 
     def put_to(ref, slot, plane0, row0):
         def put(p, h, yt, value):
@@ -621,9 +634,11 @@
                 out.append(cfd[i, h, q, :] * c[h] + total)
         return out
 
-    def finish(k, ref, slot, plane0, row0):
+    def finish(k, ref, slot, plane0, row0, between=None):
         wait_recv(exchange(k))
         install(k)
+        if between is not None:
+            between()
         for i, plane in ((0, plane0), (1, plane0 + NX - 1)):
             for t in range(4):
                 d = delta(k, i, t)
@@ -650,11 +665,6 @@
     def write_back_rest(ref, slot, plane0, row0):
         for x in range(1, NX - 1):
             write_back(x, ref, slot, plane0, row0)
-
-    def store(ref, out, index):
-        return [
-            pltpu.make_async_copy(ref.at[:, h], out.at[:, :, pl.ds(h * ZL, ZL)], load_sem.at[index, h]) for h in range(2)
-        ]
 
     wait_load(4)
     wait_load(5)
@@ -680,13 +690,13 @@
             place = (fields[n + 1], n + 1, 1, Y0)
         else:
             place = (ulast, 8, 0, 0)
-        apply(n, react, put_to(*place))
+        apply(n, n, react, put_to(*place))
         finish(n, *place)
         if n < STEPS - 1:
             start(exchange(n + 1))
+        if n == 0:
+            start(exchange(4))
         write_back_rest(*place)
-    for copy in store(ulast, out_u, 0):
-        copy.start()
 
     c_mu = 16.0 * DT * EPS_W
 
@@ -713,6 +723,32 @@
         for i in range(4):
             acc[i] = acc[i] + sums[i]
 
+    def r1(k):
+        return remote(rsend.at[k], rrecv.at[k], r1s, r1r, (lax.rem(gx + k, gx_count), gy))
+
+    def send_sums():
+        scale = -0.5 * DT / TILE**1.5
+        flat = []
+        for h in range(2):
+            s_l = jnp.broadcast_to(jnp.sum(acc[h], axis=0, keepdims=True), (8, ZL))
+            s_a = jnp.broadcast_to(jnp.sum(acc[2 + h], axis=0, keepdims=True), (8, ZL))
+            flat.append((scale * own_t[h] * s_l, scale * own_t[h] * (s_a - s_l)))
+
+        def parts_of(group):
+            ids = subf + (8 * group).astype(jnp.float32)
+            tot = []
+            for j in range(2):
+                v = sum(jnp.where(own_r[h] == ids, flat[h][j], 0.0) for h in range(2))
+                tot.append(v + pltpu.roll(v, 64, 1))
+            return jnp.where(lanes < 64, tot[0], tot[1])
+
+        rrecv[0] = parts_of(gx)
+
+        @pl.loop(1, gx_count)
+        def _(k):
+            rsend[k] = parts_of(lax.rem(gx + k, gx_count))
+            r1(k).start()
+
     for n in range(STEPS - 1, -1, -1):
         k = 4 + STEPS - 1 - n
 
@@ -730,39 +766,20 @@
             return out
 
         place = (fields[k + 1], k + 1, 1, Y0) if n > 0 else (llast, 9, 0, 0)
-        apply(k, react, put_to(*place), us[n])
-        finish(k, *place)
+        apply(k, n, react, put_to(*place), us[n])
         if n > 0:
+            finish(k, *place)
             start(exchange(k + 1))
-        write_back_rest(*place)
-        face_sums(n, k)
-    for copy in store(llast, out_lam, 1):
-        copy.start()
-
-    scale = -0.5 * DT / TILE**1.5
-    flat = []
-    for h in range(2):
-        s_l = jnp.broadcast_to(jnp.sum(acc[h], axis=0, keepdims=True), (8, ZL))
-        s_a = jnp.broadcast_to(jnp.sum(acc[2 + h], axis=0, keepdims=True), (8, ZL))
-        flat.append((scale * own_t[h] * s_l, scale * own_t[h] * (s_a - s_l)))
-
-    def parts_of(group):
-        ids = subf + (8 * group).astype(jnp.float32)
-        tot = []
-        for j in range(2):
-            v = sum(jnp.where(own_r[h] == ids, flat[h][j], 0.0) for h in range(2))
-            tot.append(v + pltpu.roll(v, 64, 1))
-        return jnp.where(lanes < 64, tot[0], tot[1])
-
-    rrecv[0] = parts_of(gx)
-
-    def r1(k):
-        return remote(rsend.at[k], rrecv.at[k], r1s, r1r, (lax.rem(gx + k, gx_count), gy))
-
-    @pl.loop(1, gx_count)
-    def _(k):
-        rsend[k] = parts_of(lax.rem(gx + k, gx_count))
-        r1(k).start()
+            write_back_rest(*place)
+            face_sums(n, k)
+        else:
+
+            def between():
+                face_sums(0, 7)
+                send_sums()
+
+            finish(k, *place, between)
+            write_back_rest(*place)
 
     wait_send(tile_copies())
     wait_send(fiber_exchange())
@@ -791,16 +808,6 @@
     for k in range(1, gy_count):
         r2(k).wait_send()
     remote(rsend.at[pl.ds(1, gx_count - 1)], rrecv.at[pl.ds(1, gx_count - 1)], r1s, r1r, (gx, gy)).wait_send()
-    for copy in store(ulast, out_u, 0) + store(llast, out_lam, 1):
-        copy.wait()
-
-
-def hand_on(u, lam, g_l, g_t, out_u, out_lam, out_l, out_t):
-    out_u[...] = u[...]
-    out_lam[...] = lam[...]
-    for j in range(2):
-        out_l[j] = g_l[j]
-        out_t[j] = g_t[j]
 
 
 def solution(mesh):
@@ -815,7 +822,7 @@
         def vmem(*shape):
             return pltpu.VMEM(shape, f32)
 
-        scratch = [padded] * 8 + [plain] * 2 + [plain] * 4 + [plain] * 2
+        scratch = [padded] * 8 + [plain] * 4 + [plain] * 2
         scratch += [
             vmem(6, NX + 2, 2, YP, ZL),
             vmem(NX + 1, 2, NY, ZL),
@@ -829,6 +836,9 @@
             padded,
             padded,
             padded,
+            vmem(NX + 1, 2, NY, ZL),
+            vmem(STEPS, NX, 2, NY, ZL),
+            vmem(STEPS, NX, 2, NY, ZL),
             vmem(10, 2, 2, YP, ZL),
             vmem(8, 4, 2, YP, ZL),
             vmem(8, 4, 2, 8, ZL),
@@ -874,24 +884,18 @@
         def body(*refs):
             kernel(gx_count, gy_count, *refs)
 
-        block = pl.BlockSpec((NX // 4, NY, 2 * ZL), lambda i: (i, 0, 0))
+        inside = pl.BlockSpec(memory_space=pltpu.VMEM)
         made = pl.pallas_call(
             body,
-            out_shape=(field, field, two, two),
+            out_shape=(pltpu.VMEM((NX, 2, NY, ZL), f32), pltpu.VMEM((NX, 2, NY, ZL), f32), two, two),
             in_specs=[any_] * 9,
-            out_specs=(any_, any_, smem, smem),
+            out_specs=(inside, inside, smem, smem),
             scratch_shapes=scratch,
             compiler_params=pltpu.CompilerParams(
-                collective_id=0, has_side_effects=True, vmem_limit_bytes=60 * 1024 * 1024
+                collective_id=0, has_side_effects=True, vmem_limit_bytes=61 * 1024 * 1024
             ),
         )(*args[:3], *args[7:], *args[3:7])
-        return pl.pallas_call(
-            hand_on,
-            grid=(4,),
-            out_shape=(field, field, two, two),
-            in_specs=[block, block, smem, smem],
-            out_specs=(block, block, smem, smem),
-        )(*made)
+        return tuple(v.transpose(0, 2, 1, 3).reshape(NX, NY, 2 * ZL) for v in made[:2]) + tuple(made[2:])
 
     return jax.shard_map(
         local,

time: 88.5 us -> 84.8 us (0.958)
  Pallas kernels: 87.7 us -> 81.5 us
  local copies, waits for them, and re-layouts: 0 us -> 2.54 us
    pallas_call x2 -> x1, Pallas kernels: 87.7 us -> 81.5 us  [local(): pl.pallas_call(body, out_shape=(pltpu.VMEM((NX, 2, NY, ZL), f32), pltpu.V...]
    reshape x0 -> x1, local copies, waits for them, and re-layouts: none -> 1.51 us  [local(): v.transpose(0, 2, 1, 3).reshape(NX, NY, 2 * ZL)]
    unnamed x0 -> x6, local copies, waits for them, and re-layouts: none -> 1.03 us
where the time goes in v3:
time: 84.8 us; the launch traced here: 84.7 us
  Pallas kernels  81.5 us (96%)
  local copies, waits for them, and re-layouts  2.54 us (3%)
    pallas_call x1, Pallas kernels, local(): pl.pallas_call(body, out_shape=(pltpu.VMEM((NX, 2, NY, ZL), f32), pltpu.V...  81.5 us

profile of v3, /device:TPU:1, one launch (start us, length us, event | category | flops | bytes accessed | tf_op | source)
XLA Modules:
  0.0 84.7 jit_solution(12537420476850519616)
XLA Ops:
  0.6 81.5 %shard_map.120 = (f32[32,2,32,128]{3,2,1,0:T(8,128)S(1)}, f32[32,2,32,128]{3,2,1,0:T(8,128)S(1)}, f32[2]{0:T(128)}, f32[2]{0:T(128)}) custom-call(f32[32,32,256]{2,1,0:T(8,128)} %refs_0_.1, f32[32,32,256]{2,1,0:T(8,128)} %refs_1_.1, f32[2,32,32,256]{3,2,1,0:T(8,128)} %refs_2_.1, f32[32,32,256]{2,1,0:T(8,128)} %refs_3_.1, f32[32,32,256]{2,1,0:T(8,128)} %refs_4_.1, ...), custom_call_target="tpu_custom_call" | custom-call | tf_op jit(solution)/shard_map/pallas_call | solution.py:888
  82.2 0.0 copy-start.1
  82.2 0.0 copy-start
  82.2 1.5 %copy_bitcast_fusion = (f32[32,32,256]{2,1,0:T(8,128)}, f32[32,32,256]{2,1,0:T(8,128)}) fusion(f32[32,2,32,128]{3,2,1,0:T(8,128)S(1)} %get-tuple-element.8, f32[32,2,32,128]{3,2,1,0:T(8,128)S(1)} %get-tuple-element.9), kind=kLoop, calls=%fused_computation | loop fusion | bytes 4194304 | tf_op jit(solution)/shard_map/reshape | solution.py:898
  83.7 0.0 copy-done.1
  83.7 0.5 copy.21
  84.2 0.0 copy-done
  84.2 0.5 copy.22
Async XLA Ops:
  82.2 1.5 %copy-start.1 = (f32[2]{0:T(128)S(1)}, f32[2]{0:T(128)}, u32[]{:S(2)}) copy-start(f32[2]{0:T(128)} %get-tuple-element.20) | copy-start | bytes 28
  82.2 2.0 %copy-start = (f32[2]{0:T(128)S(1)}, f32[2]{0:T(128)}, u32[]{:S(2)}) copy-start(f32[2]{0:T(128)} %get-tuple-element.21) | copy-start | bytes 28

commit v4 on v3

--- a/solution.py
+++ b/solution.py
@@ -123,6 +123,7 @@
     cfd,
     cfh,
     cfo,
+    kf,
     tinfo,
     trecv,
     g1send,
@@ -479,6 +480,19 @@
                     cfh[i, j, h, q, :] = c_pair * e_n * frecv[i, 1 + j, h, q, :]
                     cfo[i, j, h, Y0 + t * 8 : Y0 + t * 8 + 8, :] = ep[h] * own_products(i, 1 + j, h, t)
 
+    for i in range(4):
+        sign = -1.0 if i in (0, 2) else 1.0
+        for t in range(4):
+            q = slice(t * 8, t * 8 + 8)
+            r = Y0 + t * 8
+            turn = pair(lambda h: cfo[i, 1, h, r : r + 8, :])
+            above, below = z_up(*turn), z_down(*turn)
+            for h in range(2):
+                kf[i, 0, h, q, :] = sign * (cfh[i, 0, h, q, :] + cfo[i, 0, h, r + 1 : r + 9, :])
+                kf[i, 1, h, q, :] = sign * (cfh[i, 0, h, q, :] + cfo[i, 0, h, r - 1 : r + 7, :])
+                kf[i, 2, h, q, :] = sign * (cfh[i, 1, h, q, :] + above[h])
+                kf[i, 3, h, q, :] = sign * (cfh[i, 1, h, q, :] + below[h])
+
     for x in range(NX):
         for h in range(2):
             dy[x + 1, h, NY - 1 : NY, :] = cfd[3, h, x : x + 1, :]
@@ -494,6 +508,49 @@
         ym = pair(lambda h: f[p, h, rows(y, -1), :])
         around = (c, xp, xm, yp, ym)
         return (*around, z_up(*c), z_down(*c)) if along_z else around
+
+    def add_sums(sums, n, p, y, h, c, v, around, flux, diff):
+        q = slice(y, y + 8)
+        v_x, v_y, w_x, w_y = around
+        cross = v_x * flux[0] + v_y * flux[1] + gzs[n, p - 1, h, q, :] * flux[2]
+        m_x, m_y, m_z = diff[0] * w_x, diff[1] * w_y, diff[2] * dzs[n, p - 1, h, q, :]
+        sums[h] = sums[h] + (
+            (fhx[p, h, q, :] * m_x + fhy[p, h, q, :] * m_y) + (fp[ZZ, p, h, rows(y), :] * m_z + 0.5 * cross)
+        )
+        sums[2 + h] = sums[2 + h] + (m_x + m_y)
+        sums[4 + h] = sums[4 + h] + m_z
+        sums[6 + h] = sums[6 + h] + fp[YY, p, h, rows(y), :] * m_z
+        if h == 0:
+            m_0 = c[0] * v[0]
+            sums[8] = sums[8] + fp[ZZ, p, 0, rows(y), :] * m_0
+            sums[9] = sums[9] + m_0
+
+    def keep_sums(sums):
+        over_l = z_down(sums[6], sums[7], edge=sums[8])
+        over_t = z_down(sums[4], sums[5], edge=sums[9])
+        for h in range(2):
+            acc[h] = acc[h] + (sums[h] + over_l[h])
+            acc[2 + h] = acc[2 + h] + (2.0 * sums[2 + h] + (sums[4 + h] + over_t[h]))
+
+    def only_sums(k, n):
+        f, u = fields[k], us[n]
+
+        def body(p, carry):
+            sums = list(carry)
+            for yt in range(YT):
+                y = yt * 8
+                c, xp, xm, yp, ym, zp, zm = near(f, p, y)
+                v, vxp, vxm, vyp, vym = near(u, p, y, False)
+                for h in range(2):
+                    e_xy, e_xz, e_yz = (fp[i, p, h, rows(y), :] for i in (XY, XZ, YZ))
+                    g_x, g_y, g_z = xp[h] - xm[h], yp[h] - ym[h], zp[h] - zm[h]
+                    flux = (e_xy * g_y + e_xz * g_z, e_xy * g_x + e_yz * g_z, e_xz * g_x + e_yz * g_y)
+                    diff = (xp[h] - c[h], yp[h] - c[h], zp[h] - c[h])
+                    around = (vxp[h] - vxm[h], vyp[h] - vym[h], vxp[h] - v[h], vyp[h] - v[h])
+                    add_sums(sums, n, p, y, h, c, v, around, flux, diff)
+            return tuple(sums)
+
+        keep_sums(lax.fori_loop(1, NX + 1, body, (zero,) * 10))
 
     def stage_a(f, p, yt, react, backs, n, sens=None):
         y = yt * 8
@@ -514,22 +571,12 @@
             p_y = e_xy * g_x + e_yz * g_z
             p_z = e_xz * g_x + e_yz * g_y
             d_x, d_y, d_z = xp[h] - c[h], yp[h] - c[h], zp[h] - c[h]
-            if sens is None:
+            if sens is None and n is not None:
                 gzs[n, p - 1, h, q, :] = g_z
                 dzs[n, p - 1, h, q, :] = d_z
-            else:
-                cross = (vxp[h] - vxm[h]) * p_x + (vyp[h] - vym[h]) * p_y + gzs[n, p - 1, h, q, :] * p_z
-                m_x, m_y, m_z = d_x * (vxp[h] - v[h]), d_y * (vyp[h] - v[h]), d_z * dzs[n, p - 1, h, q, :]
-                sums[h] = sums[h] + (
-                    (fhx[p, h, q, :] * m_x + fhy[p, h, q, :] * m_y) + (fp[ZZ, p, h, rows(y), :] * m_z + 0.5 * cross)
-                )
-                sums[2 + h] = sums[2 + h] + (m_x + m_y)
-                sums[4 + h] = sums[4 + h] + m_z
-                sums[6 + h] = sums[6 + h] + fp[YY, p, h, rows(y), :] * m_z
-                if h == 0:
-                    m_0 = c[0] * v[0]
-                    sums[8] = sums[8] + fp[ZZ, p, 0, rows(y), :] * m_0
-                    sums[9] = sums[9] + m_0
+            if sens is not None:
+                around = (vxp[h] - vxm[h], vyp[h] - vym[h], vxp[h] - v[h], vyp[h] - v[h])
+                add_sums(sums, n, p, y, h, c, v, around, (p_x, p_y, p_z), (d_x, d_y, d_z))
                 p_x, p_y, p_z = ep[h] * p_x, ep[h] * p_y, ep[h] * p_z
             f_x = dx[p, h, q, :] * d_x
             f_y = dy[p, h, q, :] * d_y
@@ -574,11 +621,7 @@
         sums = lax.fori_loop(1, 3, lambda p, carry: body(p, carry, False), sums)
         sums = lax.fori_loop(3, NX + 1, body, sums)
         if u is not None:
-            over_l = z_down(sums[6], sums[7], edge=sums[8])
-            over_t = z_down(sums[4], sums[5], edge=sums[9])
-            for h in range(2):
-                acc[h] = acc[h] + (sums[h] + over_l[h])
-                acc[2 + h] = acc[2 + h] + (2.0 * sums[2 + h] + (sums[4 + h] + over_t[h]))
+            keep_sums(sums)
         for yt in range(YT):
             stage_b(NX - 1, yt, put)
         for yt in range(YT):
@@ -620,25 +663,19 @@
         q = slice(y, y + 8)
         c = pair(lambda h: halo[k, i, h, rows(y), :])
         zp, zm = z_up(*c), z_down(*c)
-        turn = pair(lambda h: cfo[i, 1, h, rows(y), :] * c[h])
-        tp, tm = z_up(*turn), z_down(*turn)
         out = []
         for h in range(2):
             bp, bm = halo[k, i, h, rows(y, 1), :], halo[k, i, h, rows(y, -1), :]
-            total = cfh[i, 0, h, q, :] * (bp - bm) + cfh[i, 1, h, q, :] * (zp[h] - zm[h])
-            total = total + (cfo[i, 0, h, rows(y, 1), :] * bp - cfo[i, 0, h, rows(y, -1), :] * bm)
-            total = total + (tp[h] - tm[h])
-            if lo:
-                out.append(cfd[i, h, q, :] * (c[h] - layer(k, i, h, rows(y))) - total)
-            else:
-                out.append(cfd[i, h, q, :] * c[h] + total)
+            total = kf[i, 0, h, q, :] * bp - kf[i, 1, h, q, :] * bm
+            total = total + (kf[i, 2, h, q, :] * zp[h] - kf[i, 3, h, q, :] * zm[h])
+            edge = c[h] - layer(k, i, h, rows(y)) if lo else c[h]
+            out.append(cfd[i, h, q, :] * edge + total)
         return out
 
-    def finish(k, ref, slot, plane0, row0, between=None):
-        wait_recv(exchange(k))
-        install(k)
-        if between is not None:
-            between()
+    def finish(k, ref, slot, plane0, row0, arrived=False):
+        if not arrived:
+            wait_recv(exchange(k))
+            install(k)
         for i, plane in ((0, plane0), (1, plane0 + NX - 1)):
             for t in range(4):
                 d = delta(k, i, t)
@@ -726,6 +763,18 @@
     def r1(k):
         return remote(rsend.at[k], rrecv.at[k], r1s, r1r, (lax.rem(gx + k, gx_count), gy))
 
+    def r2(k):
+        return remote(rg.at[0], rg.at[k], r2s.at[k], r2r.at[k], (gx, lax.rem(gy + k, gy_count)))
+
+    def second_stage():
+        rest = pl.ds(1, gx_count - 1)
+        remote(rsend.at[rest], rrecv.at[rest], r1s, r1r, (gx, gy)).wait_recv()
+        total = lax.fori_loop(0, gx_count, lambda k, t: t + rrecv[k], zero)
+        rg[0] = total
+        for k in range(1, gy_count):
+            r2(k).start()
+        return total
+
     def send_sums():
         scale = -0.5 * DT / TILE**1.5
         flat = []
@@ -766,19 +815,21 @@
             return out
 
         place = (fields[k + 1], k + 1, 1, Y0) if n > 0 else (llast, 9, 0, 0)
-        apply(k, n, react, put_to(*place), us[n])
         if n > 0:
+            apply(k, n, react, put_to(*place), us[n])
             finish(k, *place)
             start(exchange(k + 1))
             write_back_rest(*place)
             face_sums(n, k)
         else:
-
-            def between():
-                face_sums(0, 7)
-                send_sums()
-
-            finish(k, *place, between)
+            only_sums(7, 0)
+            wait_recv(exchange(7))
+            install(7)
+            face_sums(0, 7)
+            send_sums()
+            apply(k, None, react, put_to(*place))
+            total = second_stage()
+            finish(k, *place, True)
             write_back_rest(*place)
 
     wait_send(tile_copies())
@@ -789,15 +840,6 @@
         g1(k).wait_send()
     remote(quad.at[pl.ds(1, gx_count - 1)], quad.at[pl.ds(1, gx_count - 1)], g2s, g2r, (gx, gy)).wait_send()
 
-    remote(rsend.at[pl.ds(1, gx_count - 1)], rrecv.at[pl.ds(1, gx_count - 1)], r1s, r1r, (gx, gy)).wait_recv()
-    total = lax.fori_loop(0, gx_count, lambda k, s: s + rrecv[k], zero)
-    rg[0] = total
-
-    def r2(k):
-        return remote(rg.at[0], rg.at[k], r2s.at[k], r2r.at[k], (gx, lax.rem(gy + k, gy_count)))
-
-    for k in range(1, gy_count):
-        r2(k).start()
     for k in range(1, gy_count):
         r2(k).wait_recv()
         total = total + rg[k]
@@ -847,6 +889,7 @@
             vmem(4, 2, NX, ZL),
             vmem(4, 2, 2, NX, ZL),
             vmem(4, 2, 2, YP, ZL),
+            vmem(4, 4, 2, NX, ZL),
             vmem(8, ZL),
             vmem(4, 8, ZL),
             vmem(8, ZL),

time: 84.8 us -> 84.4 us (level)
  no operation moved by 1% of the time
where the time goes in v4:
time: 84.4 us; the launch traced here: 84.3 us
  Pallas kernels  81.1 us (96%)
  local copies, waits for them, and re-layouts  2.54 us (3%)
    pallas_call x1, Pallas kernels, local(): pl.pallas_call(body, out_shape=(pltpu.VMEM((NX, 2, NY, ZL), f32), pltpu.V...  81.1 us

profile of v4, /device:TPU:1, one launch (start us, length us, event | category | flops | bytes accessed | tf_op | source)
XLA Modules:
  0.0 84.3 jit_solution(7132916899901100518)
XLA Ops:
  0.6 81.1 %shard_map.120 = (f32[32,2,32,128]{3,2,1,0:T(8,128)S(1)}, f32[32,2,32,128]{3,2,1,0:T(8,128)S(1)}, f32[2]{0:T(128)}, f32[2]{0:T(128)}) custom-call(f32[32,32,256]{2,1,0:T(8,128)} %refs_0_.1, f32[32,32,256]{2,1,0:T(8,128)} %refs_1_.1, f32[2,32,32,256]{3,2,1,0:T(8,128)} %refs_2_.1, f32[32,32,256]{2,1,0:T(8,128)} %refs_3_.1, f32[32,32,256]{2,1,0:T(8,128)} %refs_4_.1, ...), custom_call_target="tpu_custom_call" | custom-call | tf_op jit(solution)/shard_map/pallas_call | solution.py:931
  81.8 0.0 copy-start.1
  81.8 0.0 copy-start
  81.8 1.5 %copy_bitcast_fusion = (f32[32,32,256]{2,1,0:T(8,128)}, f32[32,32,256]{2,1,0:T(8,128)}) fusion(f32[32,2,32,128]{3,2,1,0:T(8,128)S(1)} %get-tuple-element.8, f32[32,2,32,128]{3,2,1,0:T(8,128)S(1)} %get-tuple-element.9), kind=kLoop, calls=%fused_computation | loop fusion | bytes 4194304 | tf_op jit(solution)/shard_map/reshape | solution.py:941
  83.3 0.0 copy-done.1
  83.3 0.5 copy.21
  83.8 0.0 copy-done
  83.8 0.5 copy.22
Async XLA Ops:
  81.8 1.5 %copy-start.1 = (f32[2]{0:T(128)S(1)}, f32[2]{0:T(128)}, u32[]{:S(2)}) copy-start(f32[2]{0:T(128)} %get-tuple-element.20) | copy-start | bytes 28
  81.8 2.0 %copy-start = (f32[2]{0:T(128)S(1)}, f32[2]{0:T(128)}, u32[]{:S(2)}) copy-start(f32[2]{0:T(128)} %get-tuple-element.21) | copy-start | bytes 28
